TPU v7x, 128 devices: a whole 4x4x4 slice. The times are simulated.
128 devices in a mesh: mode: 8 (over z, y_hi), slab: 16 (over x, y_lo, core).
Axes of the slice: x: 4, y: 4 (y_hi: 2, y_lo: 2; y = y_hi * 2 + y_lo), z: 4, core: 2. Of those that a mesh axis runs over, the one named last changes fastest.
Arguments:
- modes: bfloat16 [48, 3, 32, 256, 128], P('mode', None, 'slab'), may hold values from -100 to 100
- volume: float32 [32, 256, 128], P(None, ('mode', 'slab')), may hold values from 0.5 to 24
Outputs:
- convective: float32 [2304, 48], P(('mode', 'slab'))
- dissipation: float32 [48, 48], replicated
All inputs are finite; a program needn't handle non-finite values.
Results may differ from a plain program's by a relative error of at most 0.0043.
Values may be sent and summed in bfloat16 or wider, within the bound.
A program may use at most 128 MiB of HBM per device.

v0:
```python
import math

import jax
import jax.numpy as jnp
from jax import lax
from jax.sharding import PartitionSpec as P

viscosity = 0.05


def extended(block, sides, width):
    for axis, dim in sides:
        count = lax.axis_size(axis)
        forward = [(i, i + 1) for i in range(count - 1)]
        backward = [(target, source) for source, target in forward]
        low = lax.ppermute(
            lax.slice_in_dim(block, block.shape[dim] - width, None, axis=dim), axis, forward
        )
        high = lax.ppermute(lax.slice_in_dim(block, 0, width, axis=dim), axis, backward)
        block = jnp.concatenate([low, block, high], axis=dim)
    return block


def stencil(padded, dim, length):
    shifted = [
        lax.slice_in_dim(padded, offset, offset + length, axis=dim).astype(jnp.float32)
        for offset in range(5)
    ]
    return (shifted[0] - 8.0 * shifted[1] + 8.0 * shifted[3] - shifted[4]) / 12.0


def gradient_fields(centre, x_padded, y_padded):
    z_padded = jnp.concatenate([centre[..., -2:], centre, centre[..., :2]], axis=4)
    along_x = stencil(x_padded, 2, centre.shape[2])
    along_y = stencil(y_padded, 3, centre.shape[3])
    along_z = stencil(z_padded, 4, centre.shape[4])
    return jnp.stack([along_x, along_y, along_z], axis=2).astype(jnp.bfloat16)


def regroup(stacked):
    return lax.all_to_all(
        lax.all_to_all(stacked, "mode", split_axis=3, concat_axis=0, tiled=True),
        "slab",
        split_axis=3,
        concat_axis=2,
        tiled=True,
    )


def contract(values, grad_all, weights, limit):
    mode_count = values.shape[0]
    cell_count = weights.size
    block_size = math.gcd(cell_count, limit)
    flat_values = values.reshape(mode_count, 3, cell_count)
    flat_grads = grad_all.reshape(mode_count, 3, 3, cell_count)
    flat_weights = weights.reshape(cell_count)

    def one_step(number, running):
        first_cell = number * block_size
        piece_values = lax.dynamic_slice_in_dim(flat_values, first_cell, block_size, 2)
        piece_grads = lax.dynamic_slice_in_dim(flat_grads, first_cell, block_size, 3)
        piece_weights = lax.dynamic_slice_in_dim(flat_weights, first_cell, block_size, 0)
        values_wide = piece_values.astype(jnp.float32)
        grads_wide = piece_grads.astype(jnp.float32)
        carried = values_wide[:, None, None, 0, :] * grads_wide[None, :, :, 0, :]
        carried = carried + values_wide[:, None, None, 1, :] * grads_wide[None, :, :, 1, :]
        carried = carried + values_wide[:, None, None, 2, :] * grads_wide[None, :, :, 2, :]
        carried = (
            (carried * piece_weights)
            .astype(jnp.bfloat16)
            .reshape(mode_count * mode_count, 3 * block_size)
        )
        conv_add = lax.dot_general(
            piece_values.reshape(mode_count, 3 * block_size),
            carried,
            (((1,), (1,)), ((), ())),
            preferred_element_type=jnp.float32,
        )
        weighted = (
            (grads_wide * piece_weights).astype(jnp.bfloat16).reshape(mode_count, 9 * block_size)
        )
        diss_add = lax.dot_general(
            piece_grads.reshape(mode_count, 9 * block_size),
            weighted,
            (((1,), (1,)), ((), ())),
            preferred_element_type=jnp.float32,
        )
        return (running[0] + conv_add, running[1] + diss_add)

    start_conv = jnp.zeros((mode_count, mode_count * mode_count), jnp.float32)
    start_diss = jnp.zeros((mode_count, mode_count), jnp.float32)
    conv_sum, diss_sum = lax.fori_loop(
        0, cell_count // block_size, one_step, (start_conv, start_diss)
    )
    return (conv_sum.reshape(mode_count * mode_count, mode_count), diss_sum)


def per_device(modes, volume):
    x_padded = extended(modes, (("slab", 2),), 2)
    y_padded = jnp.pad(modes, ((0, 0), (0, 0), (0, 0), (2, 2), (0, 0)))
    local_grads = gradient_fields(modes, x_padded, y_padded)
    local_count = modes.shape[0]
    stacked = jnp.concatenate(
        [modes, local_grads.reshape((local_count, 9) + modes.shape[2:])], axis=1
    )
    regrouped = regroup(stacked)
    values = regrouped[:, :3]
    grad_all = regrouped[:, 3:].reshape((regrouped.shape[0], 3, 3) + regrouped.shape[2:])
    conv_part, diss_part = contract(values, grad_all, volume, 1024)
    conv_sum = lax.psum_scatter(conv_part, ("mode", "slab"), scatter_dimension=0, tiled=True)
    diss_sum = lax.psum(diss_part, ("mode", "slab"))
    cell_total = (
        volume.shape[0]
        * volume.shape[1]
        * volume.shape[2]
        * lax.axis_size("mode")
        * lax.axis_size("slab")
    )
    convective = conv_sum * (1.0 / math.sqrt(cell_total))
    dissipation = diss_sum * (viscosity / cell_total)
    return (convective, dissipation)


def solution(mesh):
    placed = (P("mode", None, "slab", None, None), P(None, ("mode", "slab"), None))
    return jax.shard_map(
        per_device,
        mesh=mesh,
        in_specs=placed,
        out_specs=(P(("mode", "slab"), None), P()),
        check_vma=False,
    )
```

profile of v0, /device:TPU:33, one launch (start us, length us, event | category | flops | bytes accessed | tf_op | source)
XLA Modules:
  0.0 1074.8 jit_solution(17785046774700136053)
XLA Ops:
  16.3 21.5 %collective-permute-done.1 = bf16[6,3,2,256,128]{4,3,2,1,0:T(8,128)(2,1)S(1)} collective-permute-done((bf16[6,3,2,256,128]{4,3,2,1,0:T(8,128)(2,1)}, bf16[6,3,2,256,128]{4,3,2,1,0:T(8,128)(2,1)S(1)}, u32[]{:S(2)}, u32[]{:S(2)}) %collective-permute-start.1) | collective-permute-done | bytes 2359328 | tf_op jit(solution)/shard_map/ppermute | solution.py:19
  37.8 25.6 %collective-permute-done = bf16[6,3,2,256,128]{4,3,2,1,0:T(8,128)(2,1)S(1)} collective-permute-done((bf16[6,3,2,256,128]{4,3,2,1,0:T(8,128)(2,1)}, bf16[6,3,2,256,128]{4,3,2,1,0:T(8,128)(2,1)S(1)}, u32[]{:S(2)}, u32[]{:S(2)}) %collective-permute-start) | collective-permute-done | bytes 2359328 | tf_op jit(solution)/shard_map/ppermute | solution.py:16
  84.3 17.6 %copy.54 = bf16[6,12,2,256,128]{4,2,1,0,3:T(2,128)(2,1)S(1)} copy(bf16[6,12,2,256,128]{4,3,2,1,0:T(8,128)(2,1)} %pad_maximum_fusion) | data formatting | bytes 18874368 | tf_op jit(solution)/shard_map/concatenate | solution.py:103
  101.9 67.3 %all_to_all.36 = bf16[6,12,2,256,128]{4,2,1,0,3:T(2,128)(2,1)} all-to-all(bf16[6,12,2,256,128]{4,2,1,0,3:T(2,128)(2,1)S(1)} %copy.54), channel_id=1, replica_groups=mesh['mode'=8,'slab'=16] {'mode'}, dimensions={3} | all-to-all | bytes 18874368 | tf_op jit(solution)/shard_map/all_to_all | solution.py:42
  179.1 10.4 copy.56
  189.5 14.8 %copy.57 = bf16[48,12,2,32,128]{4,2,1,0,3:T(2,128)(2,1)} copy(bf16[48,12,2,32,128]{4,3,2,1,0:T(8,128)(2,1)} %bitcast.74) | data formatting | bytes 18874368 | tf_op jit(solution)/shard_map/all_to_all | solution.py:42
  204.3 29.7 %all-to-all-start.1 = ((bf16[48,12,2,32,128]{4,2,1,0,3:T(2,128)(2,1)}), bf16[48,12,2,32,128]{4,2,1,0,3:T(2,128)(2,1)}, u32[]{:S(2)}, u32[]{:S(2)}) async-start(bf16[48,12,2,32,128]{4,2,1,0,3:T(2,128)(2,1)} %copy.57), calls=%async_computation.1 | async-start | bytes 18874368 | tf_op jit(solution)/shard_map/all_to_all | solution.py:41
  234.3 143.3 %all-to-all-done.1 = bf16[48,12,2,32,128]{4,2,1,0,3:T(2,128)(2,1)} async-done(((bf16[48,12,2,32,128]{4,2,1,0,3:T(2,128)(2,1)}), bf16[48,12,2,32,128]{4,2,1,0,3:T(2,128)(2,1)}, u32[]{:S(2)}, u32[]{:S(2)}) %all-to-all-start.1) | async-done | bytes 9437216 | tf_op jit(solution)/shard_map/all_to_all | solution.py:41
  387.0 10.3 copy.59
  413.1 16.2 %reshape_reshape.3 = bf16[48,3,3,8192]{3,0,2,1:T(8,128)(2,1)} reshape(bf16[48,9,32,2,128]{4,3,2,0,1:T(2,128)(2,1)} %copy.61) | data formatting | bytes 14155776 | tf_op jit(solution)/shard_map/reshape;reshape | solution.py:55
  439.5 407.7 %while.16 = (s32[]{:T(128)}, f32[48,2304]{1,0:T(8,128)}, f32[48,48]{1,0:T(8,128)S(1)}, bf16[48,3,8192]{2,1,0:T(4,128)(2,1)}, bf16[48,3,3,8192]{3,0,2,1:T(8,128)(...) while((s32[]{:T(128)}, f32[48,2304]{1,0:T(8,128)}, ...), condition=%wide.region_1.2_spmd.clone, body=%wide.region_0.1_spmd.clone.sunk | while | flops 773485056 | bytes 75239088 | solution.py:92
  450.0 19.9 %multiply_convert_fusion.9 = bf16[48,48,3,1024]{3,2,1,0:T(4,128)(2,1)S(1)} fusion(f32[1024]{0:T(1024)S(1)} %dynamic_slice.40, f32[48,3,1024]{2,1,0:T(4,128)} %copy.84, f32[48,1024]{1,0:T(8,128)} %get-tuple-element.238, f32[48,3,1024]{2,1,0:T(4,128)} %copy.85, f32[48,1024]{1,0:T(8,128)} %get-tuple-element.240, f32[48,3,1024]{2,1,0:T(4,128)} %copy.86, ...), kind=kLoop, calls=%fused_computation.clone.1 | loop fusion | flops 49545216 | bytes 16519168 | tf_op jit(solution)/shard_map/while/body/eval_jaxpr/convert_element_type | solution.py:70
  469.9 10.4 copy.88
  501.0 19.9 %multiply_convert_fusion.9 = bf16[48,48,3,1024]{3,2,1,0:T(4,128)(2,1)S(1)} fusion(f32[1024]{0:T(1024)S(1)} %dynamic_slice.40, f32[48,3,1024]{2,1,0:T(4,128)} %copy.84, f32[48,1024]{1,0:T(8,128)} %get-tuple-element.238, f32[48,3,1024]{2,1,0:T(4,128)} %copy.85, f32[48,1024]{1,0:T(8,128)} %get-tuple-element.240, f32[48,3,1024]{2,1,0:T(4,128)} %copy.86, ...), kind=kLoop, calls=%fused_computation.clone.1 | loop fusion | flops 49545216 | bytes 16519168 | tf_op jit(solution)/shard_map/while/body/eval_jaxpr/convert_element_type | solution.py:70
  520.9 10.4 copy.88
  551.9 19.9 %multiply_convert_fusion.9 = bf16[48,48,3,1024]{3,2,1,0:T(4,128)(2,1)S(1)} fusion(f32[1024]{0:T(1024)S(1)} %dynamic_slice.40, f32[48,3,1024]{2,1,0:T(4,128)} %copy.84, f32[48,1024]{1,0:T(8,128)} %get-tuple-element.238, f32[48,3,1024]{2,1,0:T(4,128)} %copy.85, f32[48,1024]{1,0:T(8,128)} %get-tuple-element.240, f32[48,3,1024]{2,1,0:T(4,128)} %copy.86, ...), kind=kLoop, calls=%fused_computation.clone.1 | loop fusion | flops 49545216 | bytes 16519168 | tf_op jit(solution)/shard_map/while/body/eval_jaxpr/convert_element_type | solution.py:70
  571.8 10.4 copy.88
  582.2 10.1 convolution_add_fusion.2
  602.9 19.9 %multiply_convert_fusion.9 = bf16[48,48,3,1024]{3,2,1,0:T(4,128)(2,1)S(1)} fusion(f32[1024]{0:T(1024)S(1)} %dynamic_slice.40, f32[48,3,1024]{2,1,0:T(4,128)} %copy.84, f32[48,1024]{1,0:T(8,128)} %get-tuple-element.238, f32[48,3,1024]{2,1,0:T(4,128)} %copy.85, f32[48,1024]{1,0:T(8,128)} %get-tuple-element.240, f32[48,3,1024]{2,1,0:T(4,128)} %copy.86, ...), kind=kLoop, calls=%fused_computation.clone.1 | loop fusion | flops 49545216 | bytes 16519168 | tf_op jit(solution)/shard_map/while/body/eval_jaxpr/convert_element_type | solution.py:70
  622.8 10.4 copy.88
  633.2 10.1 convolution_add_fusion.2
  654.0 19.9 %multiply_convert_fusion.9 = bf16[48,48,3,1024]{3,2,1,0:T(4,128)(2,1)S(1)} fusion(f32[1024]{0:T(1024)S(1)} %dynamic_slice.40, f32[48,3,1024]{2,1,0:T(4,128)} %copy.84, f32[48,1024]{1,0:T(8,128)} %get-tuple-element.238, f32[48,3,1024]{2,1,0:T(4,128)} %copy.85, f32[48,1024]{1,0:T(8,128)} %get-tuple-element.240, f32[48,3,1024]{2,1,0:T(4,128)} %copy.86, ...), kind=kLoop, calls=%fused_computation.clone.1 | loop fusion | flops 49545216 | bytes 16519168 | tf_op jit(solution)/shard_map/while/body/eval_jaxpr/convert_element_type | solution.py:70
  673.8 10.4 copy.88
  704.9 19.9 %multiply_convert_fusion.9 = bf16[48,48,3,1024]{3,2,1,0:T(4,128)(2,1)S(1)} fusion(f32[1024]{0:T(1024)S(1)} %dynamic_slice.40, f32[48,3,1024]{2,1,0:T(4,128)} %copy.84, f32[48,1024]{1,0:T(8,128)} %get-tuple-element.238, f32[48,3,1024]{2,1,0:T(4,128)} %copy.85, f32[48,1024]{1,0:T(8,128)} %get-tuple-element.240, f32[48,3,1024]{2,1,0:T(4,128)} %copy.86, ...), kind=kLoop, calls=%fused_computation.clone.1 | loop fusion | flops 49545216 | bytes 16519168 | tf_op jit(solution)/shard_map/while/body/eval_jaxpr/convert_element_type | solution.py:70
  724.8 10.4 copy.88
  755.8 19.9 %multiply_convert_fusion.9 = bf16[48,48,3,1024]{3,2,1,0:T(4,128)(2,1)S(1)} fusion(f32[1024]{0:T(1024)S(1)} %dynamic_slice.40, f32[48,3,1024]{2,1,0:T(4,128)} %copy.84, f32[48,1024]{1,0:T(8,128)} %get-tuple-element.238, f32[48,3,1024]{2,1,0:T(4,128)} %copy.85, f32[48,1024]{1,0:T(8,128)} %get-tuple-element.240, f32[48,3,1024]{2,1,0:T(4,128)} %copy.86, ...), kind=kLoop, calls=%fused_computation.clone.1 | loop fusion | flops 49545216 | bytes 16519168 | tf_op jit(solution)/shard_map/while/body/eval_jaxpr/convert_element_type | solution.py:70
  775.7 10.4 copy.88
  806.8 19.9 %multiply_convert_fusion.9 = bf16[48,48,3,1024]{3,2,1,0:T(4,128)(2,1)S(1)} fusion(f32[1024]{0:T(1024)S(1)} %dynamic_slice.40, f32[48,3,1024]{2,1,0:T(4,128)} %copy.84, f32[48,1024]{1,0:T(8,128)} %get-tuple-element.238, f32[48,3,1024]{2,1,0:T(4,128)} %copy.85, f32[48,1024]{1,0:T(8,128)} %get-tuple-element.240, f32[48,3,1024]{2,1,0:T(4,128)} %copy.86, ...), kind=kLoop, calls=%fused_computation.clone.1 | loop fusion | flops 49545216 | bytes 16519168 | tf_op jit(solution)/shard_map/while/body/eval_jaxpr/convert_element_type | solution.py:70
  826.7 10.4 copy.88
  837.1 10.1 convolution_add_fusion.2
  847.2 70.4 %psum.7 = f32[48,48]{1,0:T(8,128)S(1)} all-reduce(f32[48,48]{1,0:T(8,128)S(1)} %get-tuple-element.113), channel_id=1, replica_groups=mesh['mode'=8,'slab'=16] {'mode','slab'}, use_global_device_ids=true, to_apply=%region_3.4 | all-reduce | flops 2304 | bytes 18432 | tf_op jit(solution)/shard_map/psum | solution.py:111
  921.0 145.6 %all-reduce.4.cloned.1.call-done = f32[2304,48]{1,0:T(8,128)} async-done(((f32[2304,48]{1,0:T(8,128)}), f32[2304,48]{1,0:T(8,128)}) %all-reduce.4.cloned.1.call-update) | async-done | bytes 442384
  (123 shorter events, 215.1 us)
Async XLA Ops:
  7.2 56.2 %copy-start = (bf16[6,3,2,256,128]{4,3,2,1,0:T(8,128)(2,1)S(1)}, bf16[6,3,2,256,128]{4,3,2,1,0:T(8,128)(2,1)}, u32[]{:S(2)}) copy-start(bf16[6,3,2,256,128]{4,3,2,1,0:T(8,128)(2,1)} %param.4) | copy-start | bytes 7077892
  7.2 30.6 %collective-permute-start.1 = (bf16[6,3,2,256,128]{4,3,2,1,0:T(8,128)(2,1)}, bf16[6,3,2,256,128]{4,3,2,1,0:T(8,128)(2,1)S(1)}, u32[]{:S(2)}, u32[]{:S(2)}) collective-permute-start(bf16[6,3,2,256,128]{4,3,2,1,0:T(8,128)(2,1)} %param.4), channel_id=1, source_target_pairs={{1,0},{2,1},{3,2},{4,3},{5,4},{6,5},{7,6},{8,7},{9,8},{10,9},{11,1... | collective-permute-start | bytes 7077896 | tf_op jit(solution)/shard_map/ppermute | solution.py:19
  9.9 53.5 %collective-permute-start = (bf16[6,3,2,256,128]{4,3,2,1,0:T(8,128)(2,1)}, bf16[6,3,2,256,128]{4,3,2,1,0:T(8,128)(2,1)S(1)}, u32[]{:S(2)}, u32[]{:S(2)}) collective-permute-start(bf16[6,3,2,256,128]{4,3,2,1,0:T(8,128)(2,1)} %param.4), channel_id=1, source_target_pairs={{0,1},{1,2},{2,3},{3,4},{4,5},{5,6},{6,7},{7,8},{8,9},{9,10},{10,1... | collective-permute-start | bytes 7077896 | tf_op jit(solution)/shard_map/ppermute | solution.py:16
  204.3 173.3 %all-to-all-start.1 = ((bf16[48,12,2,32,128]{4,2,1,0,3:T(2,128)(2,1)}), bf16[48,12,2,32,128]{4,2,1,0,3:T(2,128)(2,1)}, u32[]{:S(2)}, u32[]{:S(2)}) async-start(bf16[48,12,2,32,128]{4,2,1,0,3:T(2,128)(2,1)} %copy.57), calls=%async_computation.1 | async-start | bytes 18874368 | tf_op jit(solution)/shard_map/all_to_all | solution.py:41
  234.0 832.6 %all-reduce.4.cloned.1.call-start = ((), (), s32[]{:S(2)}) async-start(), calls=%async_computation.2 | async-start | bytes 2359296
Sparse Core Ops, SparseCore 0:
  920.5 146.0 all-reduce.3
where the time goes:
time: 1080 us; the launch traced here: 1070 us
  waiting for transfers between devices  336 us (31%)
  local copies, waits for them, and re-layouts  262 us (24%)
  other arithmetic  193 us (18%)
  blocking collectives  138 us (13%)
  matrix products  95.8 us (9%)
  starting transfers between devices  35.8 us (3%)
  between operations  14.1 us (1%)
    convert_element_type x8, other arithmetic, one_step(): carried = (carried * piece_weights).astype(jnp.bfloat16).reshape(mode_cou...  159 us
    unnamed x2, waiting for transfers between devices  146 us
    all_to_all x1, waiting for transfers between devices, regroup(): lax.all_to_all(lax.all_to_all(stacked, 'mode', split_axis=3, concat_axis=...  143 us
    while x32, local copies, waits for them, and re-layouts  90.8 us
    dot_general x8, matrix products, one_step(): lax.dot_general(piece_values.reshape(mode_count, 3 * block_size), carried...  81 us
    psum x1, blocking collectives, per_device(): diss_sum = lax.psum(diss_part, ('mode', 'slab'))  70.4 us
    all_to_all x1, blocking collectives, regroup(): lax.all_to_all(stacked, 'mode', split_axis=3, concat_axis=0, tiled=True)  67.3 us
    all_to_all x3, local copies, waits for them, and re-layouts, regroup(): lax.all_to_all(stacked, 'mode', split_axis=3, concat_axis=0, tiled=True)  35.1 us
  transfers between devices with their start and end apart: 4, of which 4 were waited for; matrix products, arithmetic and copies ran while one was open for 0% of the time, Pallas kernels for 0%

commit v1 on v0

v1 whole, which is shorter than its diff:
```python
import math

import jax
import jax.numpy as jnp
from jax import lax
from jax.experimental import pallas as pl
from jax.experimental.pallas import tpu as pltpu
from jax.sharding import PartitionSpec as P

viscosity = 0.05
bf16 = jnp.bfloat16
f32 = jnp.float32
MESH = pl.DeviceIdType.MESH
NT = (((1,), (1,)), ((), ()))
GROUP = 16


def place():
    m = lax.axis_index("mode")
    s = lax.axis_index("slab")
    return s // 4, (m % 2) * 2 + (s % 4) // 2, m // 2, s % 2


def device(x, y, z, core):
    return (z * 2 + y // 2, x * 4 + (y % 2) * 2 + core)


def block_of(y, z, core):
    return 2 * (y * 4 + z + (y % 2) * (3 - 2 * z)) + core


def owner_of(q):
    step = q // 2
    y = step // 4
    along = step % 4
    return y, along + (y % 2) * (3 - 2 * along), q % 2


def main_kernel(
    modes, volume, conv, diss, recv, vrecv, uc, wide, g, gw, uv,
    send_sem, recv_sem, vsend_sem, vrecv_sem, hsend_sem, hrecv_sem, own_sem,
):
    x, y, z, core = place()
    m = lax.axis_index("mode")
    s = lax.axis_index("slab")
    t = s % 4
    q = block_of(y, z, core)
    number = m * 16 + s

    def peer(off, sign):
        dz, dy, dc = off % 4, (off // 4) % 4, off // 16
        return (y + sign * dy + 4) % 4, (z + sign * dz + 4) % 4, (core + dc) % 2

    def home(index):
        return (index,) + owner_of(4 * m + s // 4)

    def number_of(place_):
        ids = device(*place_)
        return ids[0] * 16 + ids[1]

    def source(part):
        return (q // 4, (q % 4) * 4 + part)

    up, down = q + 1, q - 1
    neighbours = (
        (x > 0, (x - 1, y, z, core)),
        (x < 3, (x + 1, y, z, core)),
        (q > 0, (x,) + owner_of((q + 31) % 32)),
        (q < 31, (x,) + owner_of((q + 1) % 32)),
    )

    barrier = pltpu.get_barrier_semaphore()

    def greet(off, _):
        pl.semaphore_signal(
            barrier, inc=1, device_id=device(x, *peer(off, 1)), device_id_type=MESH
        )
        return 0

    lax.fori_loop(1, 32, greet, 0)
    count = 31
    for inside, other in neighbours[:2]:

        @pl.when(inside)
        def _():
            pl.semaphore_signal(barrier, inc=1, device_id=device(*other), device_id_type=MESH)

        count = count + inside.astype(jnp.int32)
    for index in range(4):
        target = home(index)
        other = number_of(target) != number

        @pl.when(other)
        def _():
            pl.semaphore_signal(barrier, inc=1, device_id=device(*target), device_id_type=MESH)

        origin = source(index)
        foreign = origin[0] * 16 + origin[1] != number

        @pl.when(foreign)
        def _():
            pl.semaphore_signal(barrier, inc=1, device_id=origin, device_id_type=MESH)

        count = count + other.astype(jnp.int32) + foreign.astype(jnp.int32)
    pl.semaphore_wait(barrier, count)

    def copy_out(off):
        py, pz, pc = peer(off, 1)
        rows = pl.multiple_of(8 * block_of(py, pz, pc), 8)
        return pltpu.make_async_remote_copy(
            src_ref=modes.at[:, :, :, pl.ds(rows, 8), :],
            dst_ref=recv.at[m, t],
            send_sem=send_sem.at[off],
            recv_sem=recv_sem.at[off],
            device_id=device(x, py, pz, pc),
            device_id_type=MESH,
        )

    def copy_in(off):
        py, pz, pc = peer(off, -1)
        slot = recv.at[pz * 2 + py // 2, (py % 2) * 2 + pc]
        return pltpu.make_async_remote_copy(
            src_ref=slot,
            dst_ref=slot,
            send_sem=send_sem.at[off],
            recv_sem=recv_sem.at[off],
            device_id=device(x, py, pz, pc),
            device_id_type=MESH,
        )

    def start_out(off, _):
        copy_out(off).start()
        return 0

    lax.fori_loop(1, 32, start_out, 0)
    own_rows = pl.multiple_of(8 * q, 8)
    own = pltpu.make_async_copy(
        modes.at[:, :, :, pl.ds(own_rows, 8), :], recv.at[m, t], own_sem.at[0]
    )
    own.start()

    def volume_out(index):
        return pltpu.make_async_remote_copy(
            src_ref=volume.at[pl.ds(8 * index, 8)],
            dst_ref=vrecv.at[t],
            send_sem=vsend_sem.at[index],
            recv_sem=vrecv_sem.at[t],
            device_id=device(*home(index)),
            device_id_type=MESH,
        )

    def volume_own():
        return pltpu.make_async_copy(volume.at[pl.ds(8 * x, 8)], vrecv.at[t], own_sem.at[1])

    def volume_in(part):
        return pltpu.make_async_remote_copy(
            src_ref=vrecv.at[part],
            dst_ref=vrecv.at[part],
            send_sem=vsend_sem.at[0],
            recv_sem=vrecv_sem.at[part],
            device_id=source(part),
            device_id_type=MESH,
        )

    own_volume = number_of(home(x)) == number
    for index in range(4):
        other = number_of(home(index)) != number

        @pl.when(other)
        def _():
            volume_out(index).start()

    @pl.when(own_volume)
    def _():
        volume_own().start()

    def wait_in(off, _):
        copy_in(off).wait_recv()
        return 0

    lax.fori_loop(1, 32, wait_in, 0)
    own.wait()

    def turn(n, _):
        a = n // 8
        plane = n % 8
        wide[...] = recv[:, plane // 2, :, a, plane % 2].astype(f32).reshape(384, 128)
        for row in range(8):
            uc[a, plane + 2, row + 2] = wide[pl.ds(row, 48, stride=8), :].astype(bf16)
        return 0

    lax.fori_loop(0, 24, turn, 0)

    sent = (
        uc.at[:, 2:4, 2:10],
        uc.at[:, 8:10, 2:10],
        uc.at[:, 2:10, 2:4],
        uc.at[:, 2:10, 8:10],
    )
    landed = (
        uc.at[:, 10:12, 2:10],
        uc.at[:, 0:2, 2:10],
        uc.at[:, 2:10, 10:12],
        uc.at[:, 2:10, 0:2],
    )
    came_to = (1, 0, 3, 2)

    def halo_out(side):
        return pltpu.make_async_remote_copy(
            src_ref=sent[side],
            dst_ref=landed[side],
            send_sem=hsend_sem.at[side],
            recv_sem=hrecv_sem.at[side],
            device_id=device(*neighbours[side][1]),
            device_id_type=MESH,
        )

    for side in (2, 3, 0, 1):

        @pl.when(neighbours[side][0])
        def _():
            halo_out(side).start()

    for side in range(4):
        edge = landed[came_to[side]]

        @pl.when(jnp.logical_not(neighbours[side][0]))
        def _():
            edge[...] = jnp.zeros(edge.shape, bf16)

    def wait_out(off, _):
        copy_out(off).wait_send()
        return 0

    lax.fori_loop(1, 32, wait_out, 0)
    for index in range(4):
        other = number_of(home(index)) != number

        @pl.when(other)
        def _():
            volume_out(index).wait_send()

        origin = source(index)
        foreign = origin[0] * 16 + origin[1] != number

        @pl.when(foreign)
        def _():
            volume_in(index).wait_recv()

    @pl.when(own_volume)
    def _():
        volume_own().wait()

    conv[...] = jnp.zeros_like(conv)
    diss[...] = jnp.zeros_like(diss)

    def tile(xx, pair):
        for r in range(2):
            weight = vrecv[pair, xx, r, :].reshape(1, 128)
            lanes = slice(r * 128, r * 128 + 128)
            for a in range(3):

                def at(dx, dy):
                    return uc[a, xx + 2 + dx, 2 * pair + r + 2 + dy].astype(f32)

                def slope(m2, m1, p1, p2):
                    return (m2 - 8.0 * m1 + 8.0 * p1 - p2) / 12.0

                centre = at(0, 0)
                uv[a, :, lanes] = centre * weight
                slopes = (
                    slope(at(-2, 0), at(-1, 0), at(1, 0), at(2, 0)),
                    slope(at(0, -2), at(0, -1), at(0, 1), at(0, 2)),
                    slope(
                        pltpu.roll(centre, 2, 1),
                        pltpu.roll(centre, 1, 1),
                        pltpu.roll(centre, 127, 1),
                        pltpu.roll(centre, 126, 1),
                    ),
                )
                for b in range(3):
                    rounded = slopes[b].astype(bf16)
                    g[a, b, :, lanes] = rounded
                    gw[a, b * 48 : b * 48 + 48, lanes] = (rounded.astype(f32) * weight).astype(
                        bf16
                    )
        for a in range(3):
            diss[...] += lax.dot_general(
                g[a].reshape(144, 256), gw[a], NT, preferred_element_type=f32
            )
        right = jnp.concatenate(
            [
                jnp.concatenate([uc[b, xx + 2, 2 * pair + 2], uc[b, xx + 2, 2 * pair + 3]], axis=1)
                for b in range(3)
            ],
            axis=1,
        )
        for first in range(0, 48, GROUP):
            rows = []
            for i in range(first, first + GROUP):
                spread = [
                    jnp.broadcast_to(uv[a, pl.ds(i, 1), :], (16, 256)).astype(bf16)
                    for a in range(3)
                ]
                outs = []
                for b in range(3):
                    parts = []
                    for k in range(0, 48, 16):
                        parts.append(
                            spread[0] * g[0, b, k : k + 16, :]
                            + spread[1] * g[1, b, k : k + 16, :]
                            + spread[2] * g[2, b, k : k + 16, :]
                        )
                    outs.append(jnp.concatenate(parts, axis=0))
                rows.append(jnp.concatenate(outs, axis=1))
            conv[first * 48 : (first + GROUP) * 48, :] += lax.dot_general(
                jnp.concatenate(rows, axis=0), right, NT, preferred_element_type=f32
            )

    def halo_in(side):
        pltpu.make_async_remote_copy(
            src_ref=landed[came_to[side]],
            dst_ref=landed[came_to[side]],
            send_sem=hsend_sem.at[came_to[side]],
            recv_sem=hrecv_sem.at[came_to[side]],
            device_id=device(*neighbours[side][1]),
            device_id_type=MESH,
        ).wait_recv()

    def step(n, _):
        edge_x = n // 16
        spot = n % 16
        xx = jnp.where(edge_x == 1, (spot // 4) + 4 * (spot // 8), 2 + spot % 4)
        inner = (spot // 4) % 4
        pair = jnp.where(
            edge_x == 1, spot % 4, jnp.where(inner < 2, 1 + inner, 3 * (inner - 2))
        )

        @pl.when(n == 8)
        def _():
            for side in (2, 3):

                @pl.when(neighbours[side][0])
                def _():
                    halo_in(side)

        @pl.when(n == 16)
        def _():
            for side in (0, 1):

                @pl.when(neighbours[side][0])
                def _():
                    halo_in(side)

        tile(xx, pair)
        return 0

    lax.fori_loop(0, 32, step, 0)
    for side in range(4):

        @pl.when(neighbours[side][0])
        def _():
            halo_out(side).wait_send()


def project(modes, volume):
    whole = pl.BlockSpec(memory_space=pltpu.VMEM)
    apart = pl.BlockSpec(memory_space=pl.ANY)
    return pl.pallas_call(
        main_kernel,
        out_shape=(
            jax.ShapeDtypeStruct((2304, 48), f32),
            jax.ShapeDtypeStruct((144, 144), f32),
        ),
        in_specs=[apart, apart],
        out_specs=(whole, whole),
        scratch_shapes=[
            pltpu.VMEM((8, 4, 6, 3, 2, 8, 128), bf16),
            pltpu.VMEM((4, 8, 2, 128), f32),
            pltpu.VMEM((3, 12, 12, 48, 128), bf16),
            pltpu.VMEM((384, 128), f32),
            pltpu.VMEM((3, 3, 48, 256), bf16),
            pltpu.VMEM((3, 144, 256), bf16),
            pltpu.VMEM((3, 48, 256), f32),
            pltpu.SemaphoreType.DMA((32,)),
            pltpu.SemaphoreType.DMA((32,)),
            pltpu.SemaphoreType.DMA((4,)),
            pltpu.SemaphoreType.DMA((4,)),
            pltpu.SemaphoreType.DMA((4,)),
            pltpu.SemaphoreType.DMA((4,)),
            pltpu.SemaphoreType.DMA((2,)),
        ],
        compiler_params=pltpu.CompilerParams(
            collective_id=0, has_side_effects=True, vmem_limit_bytes=56 << 20
        ),
    )(modes, volume)


def reduce_kernel(
    scales, conv, diss, conv_out, diss_out, dense, pieces, rbuf, dsend, drecv,
    send_sem, recv_sem, dsend_sem, drecv_sem,
):
    x, y, z, core = place()
    me = lax.axis_index("mode") * 16 + lax.axis_index("slab")

    def ids(number):
        return (number // 16, number % 16)

    barrier = pltpu.get_barrier_semaphore()

    def greet(off, _):
        pl.semaphore_signal(
            barrier, inc=1, device_id=ids((me + off) % 128), device_id_type=MESH
        )
        return 0

    lax.fori_loop(1, 128, greet, 0)

    for i in range(24):
        left = jnp.transpose(conv[i * 48 : i * 48 + 48, :])
        right = jnp.transpose(conv[(i + 24) * 48 : (i + 24) * 48 + 48, :])
        dense[i * 48 : i * 48 + 48, :] = jnp.concatenate(
            [left, right, jnp.zeros((48, 32), f32)], axis=1
        )
    dense[1152:, :] = jnp.zeros((8, 128), f32)
    for n in range(64):
        pieces[n] = dense[18 * n : 18 * n + 24, :]
    pl.semaphore_wait(barrier, 127)

    def piece_out(off):
        target = (me + off) % 128
        return pltpu.make_async_remote_copy(
            src_ref=pieces.at[target % 64],
            dst_ref=rbuf.at[me],
            send_sem=send_sem.at[off],
            recv_sem=recv_sem.at[off],
            device_id=ids(target),
            device_id_type=MESH,
        )

    def piece_in(off):
        origin = (me + 128 - off) % 128
        return pltpu.make_async_remote_copy(
            src_ref=rbuf.at[origin],
            dst_ref=rbuf.at[origin],
            send_sem=send_sem.at[off],
            recv_sem=recv_sem.at[off],
            device_id=ids(origin),
            device_id_type=MESH,
        )

    def start_piece(off, _):
        piece_out(off).start()
        return 0

    lax.fori_loop(1, 128, start_piece, 0)

    total = diss[0:48, 0:48] + diss[48:96, 48:96] + diss[96:144, 96:144]
    here = (x, y, z, core)
    for phase, (axis, size) in enumerate(((3, 2), (0, 4), (1, 4), (2, 4))):
        dsend[phase] = total
        at = here[axis]
        copies = []
        for off in range(1, size):
            there = list(here)
            there[axis] = (at + off) % size
            copies.append(
                pltpu.make_async_remote_copy(
                    src_ref=dsend.at[phase],
                    dst_ref=drecv.at[phase, at],
                    send_sem=dsend_sem.at[phase, off],
                    recv_sem=drecv_sem.at[phase, off],
                    device_id=device(*there),
                    device_id_type=MESH,
                )
            )
        for copy in copies:
            copy.start()
        drecv[phase, at] = total
        for off in range(1, size):
            there = list(here)
            there[axis] = (at + size - off) % size
            slot = drecv.at[phase, (at + size - off) % size]
            pltpu.make_async_remote_copy(
                src_ref=slot,
                dst_ref=slot,
                send_sem=dsend_sem.at[phase, off],
                recv_sem=drecv_sem.at[phase, off],
                device_id=device(*there),
                device_id_type=MESH,
            ).wait_recv()
        for copy in copies:
            copy.wait_send()
        total = drecv[phase, 0]
        for other in range(1, size):
            total = total + drecv[phase, other]
    diss_out[...] = total * scales[1]

    rbuf[me] = pieces[me % 64]

    def wait_piece(off, _):
        piece_in(off).wait_recv()
        return 0

    lax.fori_loop(1, 128, wait_piece, 0)

    def gather(n, running):
        return running + rbuf[n]

    summed = lax.fori_loop(0, 128, gather, jnp.zeros((24, 128), f32)) * scales[0]
    shifted = pltpu.roll(summed, 80, 1)

    @pl.when(me < 64)
    def _():
        conv_out[...] = summed[:18, :48]

    @pl.when(me >= 64)
    def _():
        conv_out[...] = shifted[:18, :48]

    def wait_sent(off, _):
        piece_out(off).wait_send()
        return 0

    lax.fori_loop(1, 128, wait_sent, 0)


def scatter(scales, conv, diss):
    whole = pl.BlockSpec(memory_space=pltpu.VMEM)
    return pl.pallas_call(
        lambda *refs: reduce_kernel(scales, *refs),
        out_shape=(
            jax.ShapeDtypeStruct((18, 48), f32),
            jax.ShapeDtypeStruct((48, 48), f32),
        ),
        in_specs=[whole, whole],
        out_specs=(whole, whole),
        scratch_shapes=[
            pltpu.VMEM((1160, 128), f32),
            pltpu.VMEM((64, 24, 128), f32),
            pltpu.VMEM((128, 24, 128), f32),
            pltpu.VMEM((4, 48, 48), f32),
            pltpu.VMEM((4, 4, 48, 48), f32),
            pltpu.SemaphoreType.DMA((128,)),
            pltpu.SemaphoreType.DMA((128,)),
            pltpu.SemaphoreType.DMA((4, 4)),
            pltpu.SemaphoreType.DMA((4, 4)),
        ],
        compiler_params=pltpu.CompilerParams(
            collective_id=1, has_side_effects=True, vmem_limit_bytes=32 << 20
        ),
        name="scatter",
    )(conv, diss)


def per_device(modes, volume):
    cell_total = 32 * 256 * 128
    conv_part, diss_part = project(modes, volume)
    scales = (1.0 / math.sqrt(cell_total), viscosity / cell_total)
    return scatter(scales, conv_part, diss_part)


def solution(mesh):
    placed = (P("mode", None, "slab", None, None), P(None, ("mode", "slab"), None))
    return jax.shard_map(
        per_device,
        mesh=mesh,
        in_specs=placed,
        out_specs=(P(("mode", "slab"), None), P()),
        check_vma=False,
    )
```

time: 1080 us -> 139 us (0.13)
  the two profiles are of different devices: /device:TPU:33 before, /device:TPU:16 now
where the time goes in v1:
time: 139 us
  Pallas kernels  135 us (97%)
  local copies, waits for them, and re-layouts  3.38 us (2%)
    pallas_call x1, Pallas kernels, project(): pl.pallas_call(main_kernel, out_shape=(jax.ShapeDtypeStruct((2304, 48), f...  91.2 us
    pallas_call x1, Pallas kernels, scatter(): pl.pallas_call(lambda *refs: reduce_kernel(scales, *refs), out_shape=(jax...  43.7 us
    unnamed x6, local copies, waits for them, and re-layouts  3.38 us

profile of v1, /device:TPU:16, one launch (start us, length us, event | category | flops | bytes accessed | tf_op | source)
XLA Modules:
  0.0 138.9 jit_solution(2589735057703955661)
XLA Ops:
  0.6 91.2 %shard_map.41 = (f32[2304,48]{1,0:T(8,128)}, f32[144,144]{1,0:T(8,128)}) custom-call(bf16[6,3,2,256,128]{4,3,2,1,0:T(8,128)(2,1)} %modes.1, f32[32,2,128]{2,1,0:T(2,128)} %volume.1), custom_call_target="tpu_custom_call" | custom-call | tf_op jit(solution)/shard_map/pallas_call | solution.py:369
  91.8 0.0 copy-start
  91.8 1.3 copy-done
  93.1 0.0 copy-start.1
  93.1 0.9 copy-done.1
  94.0 43.7 %scatter.1 = (f32[18,48]{1,0:T(8,128)S(1)}, f32[48,48]{1,0:T(8,128)S(1)}) custom-call(f32[2304,48]{1,0:T(8,128)S(1)} %copy-done, f32[144,144]{1,0:T(8,128)S(1)} %copy-done.1), custom_call_target="tpu_custom_call" | custom-call | tf_op jit(solution)/shard_map/scatter/pallas_call | solution.py:530
  137.7 0.6 copy.6
  138.3 0.6 copy.7
Async XLA Ops:
  91.8 1.3 copy-start
  93.1 0.9 copy-start.1

commit v2 on v1

v2 whole, which is shorter than its diff:
```python
import math

import jax
import jax.numpy as jnp
from jax import lax
from jax.experimental import pallas as pl
from jax.experimental.pallas import tpu as pltpu
from jax.sharding import PartitionSpec as P

viscosity = 0.05
bf16 = jnp.bfloat16
f32 = jnp.float32
MESH = pl.DeviceIdType.MESH
NT = (((1,), (1,)), ((), ()))
GROUP = 24
CHUNKS = 4
ROWS = 8 // CHUNKS


def place():
    m = lax.axis_index("mode")
    s = lax.axis_index("slab")
    return s // 4, (m % 2) * 2 + (s % 4) // 2, m // 2, s % 2


def device(x, y, z, core):
    return (z * 2 + y // 2, x * 4 + (y % 2) * 2 + core)


def block_of(y, z, core):
    return 2 * (y * 4 + z + (y % 2) * (3 - 2 * z)) + core


def owner_of(q):
    step = q // 2
    y = step // 4
    along = step % 4
    return y, along + (y % 2) * (3 - 2 * along), q % 2


def unit(b, column, pair, uc, uv, vrecv, g, gw, conv, diss):
    lines = [(2 * column + plane, 2 * pair + row) for plane in range(2) for row in range(2)]
    for n, (plane, row) in enumerate(lines):
        weight = vrecv[pair, plane, n % 2, :].reshape(1, 128)
        lanes = slice(n * 128, n * 128 + 128)
        for a in range(3):

            def at(shift):
                dx, dy = (shift, 0) if b == 0 else (0, shift)
                return uc[a, plane + 2 + dx, row + 2 + dy].astype(f32)

            if b == 2:
                centre = at(0)
                m2, m1, p1, p2 = (pltpu.roll(centre, by, 1) for by in (2, 1, 127, 126))
            else:
                m2, m1, p1, p2 = at(-2), at(-1), at(1), at(2)
            slope = ((m2 - p2) + 8.0 * (p1 - m1)) / 12.0
            rounded = slope.astype(bf16)
            g[a, :, lanes] = rounded
            gw[a * 48 : a * 48 + 48, lanes] = (rounded.astype(f32) * weight).astype(bf16)
    diss[...] += lax.dot_general(g[...].reshape(144, 512), gw[...], NT, preferred_element_type=f32)
    right = jnp.concatenate([uc[b, plane + 2, row + 2] for plane, row in lines], axis=1)
    for first in range(0, 48, GROUP):
        rows = []
        for i in range(first, first + GROUP):
            spread = [
                jnp.concatenate(
                    [
                        jnp.broadcast_to(uv[a, plane, row, pl.ds(i, 1), :], (16, 128)).astype(bf16)
                        for plane, row in lines
                    ],
                    axis=1,
                )
                for a in range(3)
            ]
            parts = [
                spread[0] * g[0, k : k + 16, :]
                + spread[1] * g[1, k : k + 16, :]
                + spread[2] * g[2, k : k + 16, :]
                for k in range(0, 48, 16)
            ]
            rows.append(jnp.concatenate(parts, axis=0))
        conv[first * 48 : (first + GROUP) * 48, :] += lax.dot_general(
            jnp.concatenate(rows, axis=0), right, NT, preferred_element_type=f32
        )


def main_kernel(
    modes, volume, conv, diss, recv, vrecv, uc, uv, wide, g, gw,
    send_sem, recv_sem, vsend_sem, vrecv_sem, xsend_sem, xrecv_sem, ysend_sem, yrecv_sem, own_sem,
):
    x, y, z, core = place()
    m = lax.axis_index("mode")
    s = lax.axis_index("slab")
    t = s % 4
    q = block_of(y, z, core)
    number = m * 16 + s

    def peer(off, sign):
        dz, dy, dc = off % 4, (off // 4) % 4, off // 16
        return (y + sign * dy + 4) % 4, (z + sign * dz + 4) % 4, (core + dc) % 2

    def home(index):
        return (index,) + owner_of(4 * m + s // 4)

    def number_of(place_):
        ids = device(*place_)
        return ids[0] * 16 + ids[1]

    def source(part):
        return (q // 4, (q % 4) * 4 + part)

    neighbours = (
        (x > 0, (x - 1, y, z, core)),
        (x < 3, (x + 1, y, z, core)),
        (q > 0, (x,) + owner_of((q + 31) % 32)),
        (q < 31, (x,) + owner_of((q + 1) % 32)),
    )

    barrier = pltpu.get_barrier_semaphore()

    def greet(off, _):
        pl.semaphore_signal(
            barrier, inc=1, device_id=device(x, *peer(off, 1)), device_id_type=MESH
        )
        return 0

    lax.fori_loop(1, 32, greet, 0)
    count = 31
    for inside, other in neighbours[:2]:

        @pl.when(inside)
        def _():
            pl.semaphore_signal(barrier, inc=1, device_id=device(*other), device_id_type=MESH)

        count = count + inside.astype(jnp.int32)
    for index in range(4):
        target = home(index)
        other = number_of(target) != number

        @pl.when(other)
        def _():
            pl.semaphore_signal(barrier, inc=1, device_id=device(*target), device_id_type=MESH)

        origin = source(index)
        foreign = origin[0] * 16 + origin[1] != number

        @pl.when(foreign)
        def _():
            pl.semaphore_signal(barrier, inc=1, device_id=origin, device_id_type=MESH)

        count = count + other.astype(jnp.int32) + foreign.astype(jnp.int32)
    own_volume = number_of(home(x)) == number

    def volume_out(index):
        return pltpu.make_async_remote_copy(
            src_ref=volume.at[pl.ds(8 * index, 8)],
            dst_ref=vrecv.at[t],
            send_sem=vsend_sem.at[index],
            recv_sem=vrecv_sem.at[t],
            device_id=device(*home(index)),
            device_id_type=MESH,
        )

    def volume_own():
        return pltpu.make_async_copy(volume.at[pl.ds(8 * x, 8)], vrecv.at[t], own_sem.at[CHUNKS])

    def volume_in(part):
        return pltpu.make_async_remote_copy(
            src_ref=vrecv.at[part],
            dst_ref=vrecv.at[part],
            send_sem=vsend_sem.at[0],
            recv_sem=vrecv_sem.at[part],
            device_id=source(part),
            device_id_type=MESH,
        )

    def copy_out(chunk, off):
        py, pz, pc = peer(off, 1)
        first = pl.multiple_of(8 * block_of(py, pz, pc) + ROWS * chunk, ROWS)
        return pltpu.make_async_remote_copy(
            src_ref=modes.at[:, :, :, pl.ds(first, ROWS), :],
            dst_ref=recv.at[chunk, m, t],
            send_sem=send_sem.at[chunk, off],
            recv_sem=recv_sem.at[chunk, off],
            device_id=device(x, py, pz, pc),
            device_id_type=MESH,
        )

    def copy_in(chunk, off):
        py, pz, pc = peer(off, -1)
        slot = recv.at[chunk, pz * 2 + py // 2, (py % 2) * 2 + pc]
        return pltpu.make_async_remote_copy(
            src_ref=slot,
            dst_ref=slot,
            send_sem=send_sem.at[chunk, off],
            recv_sem=recv_sem.at[chunk, off],
            device_id=device(x, py, pz, pc),
            device_id_type=MESH,
        )

    def copy_own(chunk):
        first = pl.multiple_of(8 * q + ROWS * chunk, ROWS)
        return pltpu.make_async_copy(
            modes.at[:, :, :, pl.ds(first, ROWS), :], recv.at[chunk, m, t], own_sem.at[chunk]
        )

    @pl.when(own_volume)
    def _():
        volume_own().start()

    for chunk in range(CHUNKS):
        copy_own(chunk).start()

    edges = (uc.at[:, 0:2, 2:10], uc.at[:, 10:12, 2:10], uc.at[:, 2:10, 0:2], uc.at[:, 2:10, 10:12])
    for side in range(4):

        @pl.when(jnp.logical_not(neighbours[side][0]))
        def _():
            edges[side][...] = jnp.zeros(edges[side].shape, bf16)

    conv[...] = jnp.zeros_like(conv)
    diss[...] = jnp.zeros_like(diss)
    pl.semaphore_wait(barrier, count)

    for index in range(4):
        other = number_of(home(index)) != number

        @pl.when(other)
        def _():
            volume_out(index).start()

    def start_out(n, _):
        copy_out(n // 31, n % 31 + 1).start()
        return 0

    lax.fori_loop(0, 31 * CHUNKS, start_out, 0)

    for index in range(4):
        origin = source(index)
        foreign = origin[0] * 16 + origin[1] != number

        @pl.when(foreign)
        def _():
            volume_in(index).wait_recv()

    @pl.when(own_volume)
    def _():
        volume_own().wait()

    def x_copy(side, chunk):
        rows = pl.ds(2 + ROWS * chunk, ROWS)
        planes, there = ((2, 10), (8, 0))[side]
        return pltpu.make_async_remote_copy(
            src_ref=uc.at[:, planes : planes + 2, rows],
            dst_ref=uc.at[:, there : there + 2, rows],
            send_sem=xsend_sem.at[side, chunk],
            recv_sem=xrecv_sem.at[side, chunk],
            device_id=device(*neighbours[side][1]),
            device_id_type=MESH,
        )

    def x_arrival(side, chunk):
        rows = pl.ds(2 + ROWS * chunk, ROWS)
        there = (0, 10)[side]
        return pltpu.make_async_remote_copy(
            src_ref=uc.at[:, there : there + 2, rows],
            dst_ref=uc.at[:, there : there + 2, rows],
            send_sem=xsend_sem.at[1 - side, chunk],
            recv_sem=xrecv_sem.at[1 - side, chunk],
            device_id=device(*neighbours[side][1]),
            device_id_type=MESH,
        )

    def y_copy(side):
        rows, there = ((2, 10), (8, 0))[side]
        return pltpu.make_async_remote_copy(
            src_ref=uc.at[:, 2:10, rows : rows + 2],
            dst_ref=uc.at[:, 2:10, there : there + 2],
            send_sem=ysend_sem.at[side],
            recv_sem=yrecv_sem.at[side],
            device_id=device(*neighbours[2 + side][1]),
            device_id_type=MESH,
        )

    def y_arrival(side):
        there = (0, 10)[side]
        return pltpu.make_async_remote_copy(
            src_ref=uc.at[:, 2:10, there : there + 2],
            dst_ref=uc.at[:, 2:10, there : there + 2],
            send_sem=ysend_sem.at[1 - side],
            recv_sem=yrecv_sem.at[1 - side],
            device_id=device(*neighbours[2 + side][1]),
            device_id_type=MESH,
        )

    def work(b, column, pair):
        unit(b, column, pair, uc, uv, vrecv, g, gw, conv, diss)

    def arrive(chunk, _):
        def wait_in(off, _):
            copy_in(chunk, off).wait_recv()
            return 0

        lax.fori_loop(1, 32, wait_in, 0)
        copy_own(chunk).wait()

        def turn(n, _):
            a = n // 8
            plane = n % 8
            wide[:, 0:ROWS, :] = (
                recv[chunk, :, plane // 2, :, a, plane % 2].astype(f32).reshape(48, ROWS, 128)
            )
            for row in range(ROWS):
                here = ROWS * chunk + row
                field = wide.reshape(384, 128)[pl.ds(row, 48, stride=8), :]
                uc[a, plane + 2, here + 2] = field.astype(bf16)
                weight = vrecv[here // 2, plane, pl.ds(here % 2, 1), :].reshape(1, 128)
                uv[a, plane, here] = field * weight
            return 0

        lax.fori_loop(0, 24, turn, 0)

        for side in range(2):

            @pl.when(neighbours[side][0])
            def _():
                x_copy(side, chunk).start()

        @pl.when(jnp.logical_and(chunk == 0, neighbours[2][0]))
        def _():
            y_copy(0).start()

        @pl.when(jnp.logical_and(chunk == CHUNKS - 1, neighbours[3][0]))
        def _():
            y_copy(1).start()

        def along_z(n, _):
            work(2, n % 4, chunk * (ROWS // 2) + n // 4)
            return 0

        lax.fori_loop(0, 2 * ROWS, along_z, 0)

        def along_x(n, _):
            work(0, 1 + n % 2, chunk * (ROWS // 2) + n // 2)
            return 0

        lax.fori_loop(0, ROWS, along_x, 0)
        return 0

    lax.fori_loop(0, CHUNKS, arrive, 0)

    for side in range(2):
        for chunk in range(CHUNKS):

            @pl.when(neighbours[side][0])
            def _():
                x_arrival(side, chunk).wait_recv()

    def along_x_edge(n, _):
        work(0, 3 * (n % 2), n // 2)
        return 0

    lax.fori_loop(0, 8, along_x_edge, 0)

    def along_y(n, _):
        @pl.when(n == 8)
        def _():
            for side in range(2):

                @pl.when(neighbours[2 + side][0])
                def _():
                    y_arrival(side).wait_recv()

        half = (n // 4) % 2
        work(1, n % 4, jnp.where(n < 8, 1 + half, 3 * half))
        return 0

    lax.fori_loop(0, 16, along_y, 0)

    def wait_out(n, _):
        copy_out(n // 31, n % 31 + 1).wait_send()
        return 0

    lax.fori_loop(0, 31 * CHUNKS, wait_out, 0)
    for index in range(4):
        other = number_of(home(index)) != number

        @pl.when(other)
        def _():
            volume_out(index).wait_send()

    for side in range(2):

        @pl.when(neighbours[side][0])
        def _():
            for chunk in range(CHUNKS):
                x_copy(side, chunk).wait_send()

        @pl.when(neighbours[2 + side][0])
        def _():
            y_copy(side).wait_send()


def project(modes, volume):
    whole = pl.BlockSpec(memory_space=pltpu.VMEM)
    apart = pl.BlockSpec(memory_space=pl.ANY)
    return pl.pallas_call(
        main_kernel,
        out_shape=(
            jax.ShapeDtypeStruct((2304, 48), f32),
            jax.ShapeDtypeStruct((144, 144), f32),
        ),
        in_specs=[apart, apart],
        out_specs=(whole, whole),
        scratch_shapes=[
            pltpu.VMEM((CHUNKS, 8, 4, 6, 3, 2, ROWS, 128), bf16),
            pltpu.VMEM((4, 8, 2, 128), f32),
            pltpu.VMEM((3, 12, 12, 48, 128), bf16),
            pltpu.VMEM((3, 8, 8, 48, 128), f32),
            pltpu.VMEM((48, 8, 128), f32),
            pltpu.VMEM((3, 48, 512), bf16),
            pltpu.VMEM((144, 512), bf16),
            pltpu.SemaphoreType.DMA((CHUNKS, 32)),
            pltpu.SemaphoreType.DMA((CHUNKS, 32)),
            pltpu.SemaphoreType.DMA((4,)),
            pltpu.SemaphoreType.DMA((4,)),
            pltpu.SemaphoreType.DMA((2, CHUNKS)),
            pltpu.SemaphoreType.DMA((2, CHUNKS)),
            pltpu.SemaphoreType.DMA((2,)),
            pltpu.SemaphoreType.DMA((2,)),
            pltpu.SemaphoreType.DMA((CHUNKS + 1,)),
        ],
        compiler_params=pltpu.CompilerParams(
            collective_id=0, has_side_effects=True, vmem_limit_bytes=56 << 20
        ),
    )(modes, volume)


def reduce_kernel(
    scales, conv, diss, conv_out, diss_out, turned, pieces, rbuf, dsend, drecv,
    send_sem, recv_sem, dsend_sem, drecv_sem,
):
    x, y, z, core = place()
    me = lax.axis_index("mode") * 16 + lax.axis_index("slab")

    def ids(number):
        return (number // 16, number % 16)

    barrier = pltpu.get_barrier_semaphore()

    def greet(off, _):
        pl.semaphore_signal(
            barrier, inc=1, device_id=ids((me + off) % 128), device_id_type=MESH
        )
        return 0

    lax.fori_loop(1, 128, greet, 0)

    for i in range(48):
        turned[i * 48 : i * 48 + 48, :] = jnp.transpose(conv[i * 48 : i * 48 + 48, :])
    turned[2304:, :] = jnp.zeros((8, 48), f32)
    lane = lax.broadcasted_iota(jnp.int32, (8, 128), 1)
    line = lax.broadcasted_iota(jnp.int32, (8, 128), 0)

    def padded(first):
        return jnp.concatenate([turned[first : first + 8, :], jnp.zeros((8, 80), f32)], axis=1)

    for n in range(128):
        packed = jnp.where(lane < 48, padded(18 * n), pltpu.roll(padded(18 * n + 8), 48, 1))
        for third in range(3):
            ends = pltpu.roll(padded(18 * n + 16 - 2 * third), 96 - 16 * third, 1)
            there = (lane >= 96) & (lane < 112) & (line // 2 == third)
            packed = jnp.where(there, ends, packed)
        pieces[n] = packed
    pl.semaphore_wait(barrier, 127)

    def piece_out(off):
        target = (me + 37 * off) % 128
        return pltpu.make_async_remote_copy(
            src_ref=pieces.at[target],
            dst_ref=rbuf.at[me],
            send_sem=send_sem.at[off],
            recv_sem=recv_sem.at[off],
            device_id=ids(target),
            device_id_type=MESH,
        )

    def piece_in(off):
        origin = (me + 128 - (37 * off) % 128) % 128
        return pltpu.make_async_remote_copy(
            src_ref=rbuf.at[origin],
            dst_ref=rbuf.at[origin],
            send_sem=send_sem.at[off],
            recv_sem=recv_sem.at[off],
            device_id=ids(origin),
            device_id_type=MESH,
        )

    def start_piece(off, _):
        piece_out(off).start()
        return 0

    lax.fori_loop(1, 128, start_piece, 0)

    total = diss[0:48, 0:48] + diss[48:96, 48:96] + diss[96:144, 96:144]
    here = (x, y, z, core)
    for phase, (axis, size) in enumerate(((3, 2), (0, 4), (1, 4), (2, 4))):
        dsend[phase] = total
        at = here[axis]
        copies = []
        for off in range(1, size):
            there = list(here)
            there[axis] = (at + off) % size
            copies.append(
                pltpu.make_async_remote_copy(
                    src_ref=dsend.at[phase],
                    dst_ref=drecv.at[phase, at],
                    send_sem=dsend_sem.at[phase, off],
                    recv_sem=drecv_sem.at[phase, off],
                    device_id=device(*there),
                    device_id_type=MESH,
                )
            )
        for copy in copies:
            copy.start()
        drecv[phase, at] = total
        for off in range(1, size):
            there = list(here)
            there[axis] = (at + size - off) % size
            slot = drecv.at[phase, (at + size - off) % size]
            pltpu.make_async_remote_copy(
                src_ref=slot,
                dst_ref=slot,
                send_sem=dsend_sem.at[phase, off],
                recv_sem=drecv_sem.at[phase, off],
                device_id=device(*there),
                device_id_type=MESH,
            ).wait_recv()
        for copy in copies:
            copy.wait_send()
        total = drecv[phase, 0]
        for other in range(1, size):
            total = total + drecv[phase, other]
    diss_out[...] = total * scales[1]

    rbuf[me] = pieces[me]

    def wait_piece(off, _):
        piece_in(off).wait_recv()
        return 0

    lax.fori_loop(1, 128, wait_piece, 0)

    def gather(n, running):
        return running + rbuf[n]

    summed = lax.fori_loop(0, 128, gather, jnp.zeros((8, 128), f32)) * scales[0]
    conv_out[0:8, :] = summed[:, :48]
    conv_out[8:16, :] = pltpu.roll(summed, 80, 1)[:, :48]
    ends = jnp.zeros((8, 128), f32)
    for third in range(3):
        piece = pltpu.roll(summed, (128 - 96 + 16 * third) % 128, 1)
        piece = pltpu.roll(piece, (8 - 2 * third) % 8, 0) if third else piece
        ends = jnp.where((lane >= 16 * third) & (lane < 16 * third + 16), piece, ends)
    conv_out[16:18, :] = ends[:2, :48]

    def wait_sent(off, _):
        piece_out(off).wait_send()
        return 0

    lax.fori_loop(1, 128, wait_sent, 0)


def scatter(scales, conv, diss):
    whole = pl.BlockSpec(memory_space=pltpu.VMEM)
    return pl.pallas_call(
        lambda *refs: reduce_kernel(scales, *refs),
        out_shape=(
            jax.ShapeDtypeStruct((18, 48), f32),
            jax.ShapeDtypeStruct((48, 48), f32),
        ),
        in_specs=[whole, whole],
        out_specs=(whole, whole),
        scratch_shapes=[
            pltpu.VMEM((2312, 48), f32),
            pltpu.VMEM((128, 8, 128), f32),
            pltpu.VMEM((128, 8, 128), f32),
            pltpu.VMEM((4, 48, 48), f32),
            pltpu.VMEM((4, 4, 48, 48), f32),
            pltpu.SemaphoreType.DMA((128,)),
            pltpu.SemaphoreType.DMA((128,)),
            pltpu.SemaphoreType.DMA((4, 4)),
            pltpu.SemaphoreType.DMA((4, 4)),
        ],
        compiler_params=pltpu.CompilerParams(
            collective_id=1, has_side_effects=True, vmem_limit_bytes=32 << 20
        ),
        name="scatter",
    )(conv, diss)


def per_device(modes, volume):
    cell_total = 32 * 256 * 128
    conv_part, diss_part = project(modes, volume)
    scales = (1.0 / math.sqrt(cell_total), viscosity / cell_total)
    return scatter(scales, conv_part, diss_part)


def solution(mesh):
    placed = (P("mode", None, "slab", None, None), P(None, ("mode", "slab"), None))
    return jax.shard_map(
        per_device,
        mesh=mesh,
        in_specs=placed,
        out_specs=(P(("mode", "slab"), None), P()),
        check_vma=False,
    )
```

time: 139 us -> 112 us (0.81)
  the two profiles are of different devices: /device:TPU:16 before, /device:TPU:0 now
where the time goes in v2:
time: 112 us
  Pallas kernels  108 us (96%)
  local copies, waits for them, and re-layouts  3.38 us (3%)
    pallas_call x1, Pallas kernels, project(): pl.pallas_call(main_kernel, out_shape=(jax.ShapeDtypeStruct((2304, 48), f...  77.4 us
    pallas_call x1, Pallas kernels, scatter(): pl.pallas_call(lambda *refs: reduce_kernel(scales, *refs), out_shape=(jax...  30.5 us
    unnamed x6, local copies, waits for them, and re-layouts  3.38 us

profile of v2, /device:TPU:0, one launch (start us, length us, event | category | flops | bytes accessed | tf_op | source)
XLA Modules:
  0.0 111.9 jit_solution(2451377625326274536)
XLA Ops:
  0.6 77.4 %shard_map.41 = (f32[2304,48]{1,0:T(8,128)}, f32[144,144]{1,0:T(8,128)}) custom-call(bf16[6,3,2,256,128]{4,3,2,1,0:T(8,128)(2,1)} %modes.1, f32[32,2,128]{2,1,0:T(2,128)} %volume.1), custom_call_target="tpu_custom_call" | custom-call | tf_op jit(solution)/shard_map/pallas_call | solution.py:408
  78.0 0.0 copy-start
  78.1 1.3 %copy-done = f32[2304,48]{1,0:T(8,128)S(1)} copy-done((f32[2304,48]{1,0:T(8,128)S(1)}, f32[2304,48]{1,0:T(8,128)}, u32[]{:S(2)}) %copy-start) | copy-done | bytes 442392
  79.3 0.0 copy-start.1
  79.3 0.9 copy-done.1
  80.2 30.5 %scatter.1 = (f32[18,48]{1,0:T(8,128)S(1)}, f32[48,48]{1,0:T(8,128)S(1)}) custom-call(f32[2304,48]{1,0:T(8,128)S(1)} %copy-done, f32[144,144]{1,0:T(8,128)S(1)} %copy-done.1), custom_call_target="tpu_custom_call" | custom-call | tf_op jit(solution)/shard_map/scatter/pallas_call | solution.py:577
  110.7 0.6 copy.6
  111.3 0.6 copy.7
Async XLA Ops:
  78.0 1.3 %copy-start = (f32[2304,48]{1,0:T(8,128)S(1)}, f32[2304,48]{1,0:T(8,128)}, u32[]{:S(2)}) copy-start(f32[2304,48]{1,0:T(8,128)} %get-tuple-element.4.refs_0_) | copy-start | bytes 1327108
  79.3 0.9 copy-start.1

commit v3 on v2

v3 whole, which is shorter than its diff:
```python
import functools
import math

import jax
import jax.numpy as jnp
from jax import lax
from jax.experimental import pallas as pl
from jax.experimental.pallas import tpu as pltpu
from jax.sharding import PartitionSpec as P

viscosity = 0.05
bf16 = jnp.bfloat16
f32 = jnp.float32
MESH = pl.DeviceIdType.MESH
NT = (((1,), (1,)), ((), ()))
GROUP = 24
CHUNKS = 4
ROWS = 8 // CHUNKS
AXES = ((3, 2), (0, 4), (1, 4), (2, 4))


def place():
    m = lax.axis_index("mode")
    s = lax.axis_index("slab")
    return s // 4, (m % 2) * 2 + (s % 4) // 2, m // 2, s % 2


def device(x, y, z, core):
    return (z * 2 + y // 2, x * 4 + (y % 2) * 2 + core)


def block_of(y, z, core):
    return 2 * (y * 4 + z + (y % 2) * (3 - 2 * z)) + core


def owner_of(q):
    step = q // 2
    y = step // 4
    along = step % 4
    return y, along + (y % 2) * (3 - 2 * along), q % 2


def lines_of(column, pair):
    return [(2 * column + plane, 2 * pair + row) for plane in range(2) for row in range(2)]


def slopes(b, column, pair, uc, vrecv, g, gw):
    for n, (plane, row) in enumerate(lines_of(column, pair)):
        weight = vrecv[pair, plane, n % 2, :].reshape(1, 128)
        lanes = slice(n * 128, n * 128 + 128)
        for a in range(3):

            def at(shift):
                dx, dy = (shift, 0) if b == 0 else (0, shift)
                return uc[a, plane + 2 + dx, row + 2 + dy].astype(f32)

            if b == 2:
                centre = at(0)
                m2, m1, p1, p2 = (pltpu.roll(centre, by, 1) for by in (2, 1, 127, 126))
            else:
                m2, m1, p1, p2 = at(-2), at(-1), at(1), at(2)
            rounded = (((m2 - p2) + 8.0 * (p1 - m1)) * (1.0 / 12.0)).astype(bf16)
            g[a, :, lanes] = rounded
            gw[a * 48 : a * 48 + 48, lanes] = (rounded.astype(f32) * weight).astype(bf16)


def products(modes_i, lines, uv, g):
    rows = []
    for i in modes_i:
        spread = [
            jnp.concatenate(
                [
                    jnp.broadcast_to(uv[a, plane, row, pl.ds(i, 1), :], (16, 128)).astype(bf16)
                    for plane, row in lines
                ],
                axis=1,
            )
            for a in range(3)
        ]
        for k in range(0, 48, 16):
            rows.append(
                spread[0] * g[0, k : k + 16, :]
                + spread[1] * g[1, k : k + 16, :]
                + spread[2] * g[2, k : k + 16, :]
            )
    return jnp.concatenate(rows, axis=0)


def advected(b, lines, uc):
    return jnp.concatenate([uc[b, plane + 2, row + 2] for plane, row in lines], axis=1)


def viscous(g, gw, diss):
    diss[...] += lax.dot_general(g[...].reshape(144, 512), gw[...], NT, preferred_element_type=f32)


def contract(b, column, pair, uc, uv, g, gw, conv, diss):
    lines = lines_of(column, pair)
    right = advected(b, lines, uc)
    for first in range(0, 48, GROUP):
        conv[first * 48 : (first + GROUP) * 48, :] += lax.dot_general(
            products(range(first, first + GROUP), lines, uv, g),
            right,
            NT,
            preferred_element_type=f32,
        )
    viscous(g, gw, diss)


def four_units(b, pair, uc, uv, vrecv, g, gw, conv, diss):
    slopes(b, 0, pair, uc, vrecv, g.at[0], gw.at[0])
    for n in range(4):
        if n < 3:
            slopes(b, n + 1, pair, uc, vrecv, g.at[n + 1], gw.at[n + 1])
        contract(b, n, pair, uc, uv, g.at[n], gw.at[n], conv, diss)


def main_kernel(
    scales, modes, volume, conv_out, diss_out,
    recv, vrecv, uc, uv, wide, g, gw, last_g, conv, diss, turned, pieces, rbuf, dsend, drecv,
    send_sem, recv_sem, vsend_sem, vrecv_sem, xsend_sem, xrecv_sem, ysend_sem, yrecv_sem, own_sem,
    psend_sem, precv_sem, dsend_sem, drecv_sem, ready_sem,
):
    x, y, z, core = place()
    m = lax.axis_index("mode")
    s = lax.axis_index("slab")
    t = s % 4
    q = block_of(y, z, core)
    number = m * 16 + s

    def peer(off, sign):
        dz, dy, dc = off % 4, (off // 4) % 4, off // 16
        return (y + sign * dy + 4) % 4, (z + sign * dz + 4) % 4, (core + dc) % 2

    def home(index):
        return (index,) + owner_of(4 * m + s // 4)

    def number_of(place_):
        ids = device(*place_)
        return ids[0] * 16 + ids[1]

    def source(part):
        return (q // 4, (q % 4) * 4 + part)

    neighbours = (
        (x > 0, (x - 1, y, z, core)),
        (x < 3, (x + 1, y, z, core)),
        (q > 0, (x,) + owner_of((q + 31) % 32)),
        (q < 31, (x,) + owner_of((q + 1) % 32)),
    )

    barrier = pltpu.get_barrier_semaphore()

    def greet(off, _):
        pl.semaphore_signal(
            barrier, inc=1, device_id=device(x, *peer(off, 1)), device_id_type=MESH
        )
        return 0

    lax.fori_loop(1, 32, greet, 0)
    for step in range(1, 4):
        pl.semaphore_signal(
            barrier, inc=1, device_id=device((x + step) % 4, y, z, core), device_id_type=MESH
        )
    count = 34
    for index in range(4):
        target = home(index)
        other = number_of(target) != number

        @pl.when(other)
        def _():
            pl.semaphore_signal(barrier, inc=1, device_id=device(*target), device_id_type=MESH)

        origin = source(index)
        foreign = origin[0] * 16 + origin[1] != number

        @pl.when(foreign)
        def _():
            pl.semaphore_signal(barrier, inc=1, device_id=origin, device_id_type=MESH)

        count = count + other.astype(jnp.int32) + foreign.astype(jnp.int32)
    own_volume = number_of(home(x)) == number

    def volume_out(index):
        return pltpu.make_async_remote_copy(
            src_ref=volume.at[pl.ds(8 * index, 8)],
            dst_ref=vrecv.at[t],
            send_sem=vsend_sem.at[index],
            recv_sem=vrecv_sem.at[t],
            device_id=device(*home(index)),
            device_id_type=MESH,
        )

    def volume_own():
        return pltpu.make_async_copy(volume.at[pl.ds(8 * x, 8)], vrecv.at[t], own_sem.at[CHUNKS])

    def volume_in(part):
        return pltpu.make_async_remote_copy(
            src_ref=vrecv.at[part],
            dst_ref=vrecv.at[part],
            send_sem=vsend_sem.at[0],
            recv_sem=vrecv_sem.at[part],
            device_id=source(part),
            device_id_type=MESH,
        )

    def copy_out(chunk, off):
        py, pz, pc = peer(off, 1)
        first = pl.multiple_of(8 * block_of(py, pz, pc) + ROWS * chunk, ROWS)
        return pltpu.make_async_remote_copy(
            src_ref=modes.at[:, :, :, pl.ds(first, ROWS), :],
            dst_ref=recv.at[chunk, m, t],
            send_sem=send_sem.at[chunk, off],
            recv_sem=recv_sem.at[chunk, off],
            device_id=device(x, py, pz, pc),
            device_id_type=MESH,
        )

    def copy_in(chunk, off):
        py, pz, pc = peer(off, -1)
        slot = recv.at[chunk, pz * 2 + py // 2, (py % 2) * 2 + pc]
        return pltpu.make_async_remote_copy(
            src_ref=slot,
            dst_ref=slot,
            send_sem=send_sem.at[chunk, off],
            recv_sem=recv_sem.at[chunk, off],
            device_id=device(x, py, pz, pc),
            device_id_type=MESH,
        )

    def copy_own(chunk):
        first = pl.multiple_of(8 * q + ROWS * chunk, ROWS)
        return pltpu.make_async_copy(
            modes.at[:, :, :, pl.ds(first, ROWS), :], recv.at[chunk, m, t], own_sem.at[chunk]
        )

    @pl.when(own_volume)
    def _():
        volume_own().start()

    for chunk in range(CHUNKS):
        copy_own(chunk).start()

    edges = (uc.at[:, 0:2, 2:10], uc.at[:, 10:12, 2:10], uc.at[:, 2:10, 0:2], uc.at[:, 2:10, 10:12])
    for side in range(4):

        @pl.when(jnp.logical_not(neighbours[side][0]))
        def _():
            edges[side][...] = jnp.zeros(edges[side].shape, bf16)

    conv[...] = jnp.zeros_like(conv)
    diss[...] = jnp.zeros_like(diss)
    turned[576:, :] = jnp.zeros((8, 48), f32)
    pl.semaphore_wait(barrier, count)
    for step in range(1, 4):
        pl.semaphore_signal(
            ready_sem, inc=1, device_id=device((x + step) % 4, y, z, core), device_id_type=MESH
        )

    for index in range(4):
        other = number_of(home(index)) != number

        @pl.when(other)
        def _():
            volume_out(index).start()

    def start_out(n, _):
        copy_out(n // 31, n % 31 + 1).start()
        return 0

    lax.fori_loop(0, 31 * CHUNKS, start_out, 0)

    for index in range(4):
        origin = source(index)
        foreign = origin[0] * 16 + origin[1] != number

        @pl.when(foreign)
        def _():
            volume_in(index).wait_recv()

    @pl.when(own_volume)
    def _():
        volume_own().wait()

    def x_copy(side, chunk):
        rows = pl.ds(2 + ROWS * chunk, ROWS)
        planes, there = ((2, 10), (8, 0))[side]
        return pltpu.make_async_remote_copy(
            src_ref=uc.at[:, planes : planes + 2, rows],
            dst_ref=uc.at[:, there : there + 2, rows],
            send_sem=xsend_sem.at[side, chunk],
            recv_sem=xrecv_sem.at[side, chunk],
            device_id=device(*neighbours[side][1]),
            device_id_type=MESH,
        )

    def x_arrival(side, chunk):
        rows = pl.ds(2 + ROWS * chunk, ROWS)
        there = (0, 10)[side]
        return pltpu.make_async_remote_copy(
            src_ref=uc.at[:, there : there + 2, rows],
            dst_ref=uc.at[:, there : there + 2, rows],
            send_sem=xsend_sem.at[1 - side, chunk],
            recv_sem=xrecv_sem.at[1 - side, chunk],
            device_id=device(*neighbours[side][1]),
            device_id_type=MESH,
        )

    def y_copy(side):
        rows, there = ((2, 10), (8, 0))[side]
        return pltpu.make_async_remote_copy(
            src_ref=uc.at[:, 2:10, rows : rows + 2],
            dst_ref=uc.at[:, 2:10, there : there + 2],
            send_sem=ysend_sem.at[side],
            recv_sem=yrecv_sem.at[side],
            device_id=device(*neighbours[2 + side][1]),
            device_id_type=MESH,
        )

    def y_arrival(side):
        there = (0, 10)[side]
        return pltpu.make_async_remote_copy(
            src_ref=uc.at[:, 2:10, there : there + 2],
            dst_ref=uc.at[:, 2:10, there : there + 2],
            send_sem=ysend_sem.at[1 - side],
            recv_sem=yrecv_sem.at[1 - side],
            device_id=device(*neighbours[2 + side][1]),
            device_id_type=MESH,
        )

    def arrive(chunk):
        def wait_in(off, _):
            copy_in(chunk, off).wait_recv()
            return 0

        lax.fori_loop(1, 32, wait_in, 0)
        copy_own(chunk).wait()

        def turn(n, _):
            a = n // 8
            plane = n % 8
            wide[:, 0:ROWS, :] = (
                recv[chunk, :, plane // 2, :, a, plane % 2].astype(f32).reshape(48, ROWS, 128)
            )
            for row in range(ROWS):
                here = ROWS * chunk + row
                field = wide.reshape(384, 128)[pl.ds(row, 48, stride=8), :]
                uc[a, plane + 2, here + 2] = field.astype(bf16)
                weight = vrecv[here // 2, plane, pl.ds(here % 2, 1), :].reshape(1, 128)
                uv[a, plane, here] = field * weight
            return 0

        lax.fori_loop(0, 24, turn, 0)

        for side in range(2):

            @pl.when(neighbours[side][0])
            def _():
                x_copy(side, chunk).start()

        @pl.when(jnp.logical_and(chunk == 0, neighbours[2][0]))
        def _():
            y_copy(0).start()

        @pl.when(jnp.logical_and(chunk == CHUNKS - 1, neighbours[3][0]))
        def _():
            y_copy(1).start()

    def work(b, pair):
        four_units(b, pair, uc, uv, vrecv, g, gw, conv, diss)

    def advance(chunk, _):
        @pl.when(chunk < CHUNKS)
        def _():
            arrive(chunk)
            work(2, chunk)

        @pl.when(chunk >= 1)
        def _():
            for side in range(2):

                @pl.when(neighbours[side][0])
                def _():
                    x_arrival(side, chunk - 1).wait_recv()

            work(0, chunk - 1)

        @pl.when(jnp.logical_or(chunk == 2, chunk == 4))
        def _():
            work(1, chunk // 2)

        return 0

    lax.fori_loop(0, CHUNKS + 1, advance, 0)

    for side in range(2):

        @pl.when(neighbours[2 + side][0])
        def _():
            y_arrival(side).wait_recv()

    def last_slopes(half, _):
        for n in range(4):
            slot = last_g.at[4 * half + n]
            slopes(1, n, 3 * half, uc, vrecv, slot, gw.at[n])
            viscous(slot, gw.at[n], diss)
        return 0

    lax.fori_loop(0, 2, last_slopes, 0)

    here = (x, y, z, core)

    def viscous_copy(phase, off, sign):
        axis, size = AXES[phase]
        there = list(here)
        there[axis] = (here[axis] + sign * off + size) % size
        slot = drecv.at[phase, here[axis] if sign > 0 else there[axis]]
        return pltpu.make_async_remote_copy(
            src_ref=dsend.at[phase] if sign > 0 else slot,
            dst_ref=slot,
            send_sem=dsend_sem.at[phase, off],
            recv_sem=drecv_sem.at[phase, off],
            device_id=device(*there),
            device_id_type=MESH,
        )

    def viscous_start(phase, total):
        dsend[phase] = total
        drecv[phase, here[AXES[phase][0]]] = total
        for off in range(1, AXES[phase][1]):
            viscous_copy(phase, off, 1).start()

    def viscous_end(phase):
        size = AXES[phase][1]
        for off in range(1, size):
            viscous_copy(phase, off, -1).wait_recv()
        total = drecv[phase, 0]
        for other in range(1, size):
            total = total + drecv[phase, other]
        return total

    viscous_start(0, diss[0:48, 0:48] + diss[48:96, 48:96] + diss[96:144, 96:144])
    pl.semaphore_wait(ready_sem, 3)

    me = number
    lane = lax.broadcasted_iota(jnp.int32, (8, 128), 1)
    line = lax.broadcasted_iota(jnp.int32, (8, 128), 0)

    def padded(first):
        return jnp.concatenate([turned[first : first + 8, :], jnp.zeros((8, 80), f32)], axis=1)

    def packed(first):
        tile = jnp.where(lane < 48, padded(first), pltpu.roll(padded(first + 8), 48, 1))
        for third in range(3):
            ends = pltpu.roll(padded(first + 16 - 2 * third), 96 - 16 * third, 1)
            tile = jnp.where((lane >= 96) & (lane < 112) & (line // 2 == third), ends, tile)
        return tile

    def piece_out(target):
        return pltpu.make_async_remote_copy(
            src_ref=pieces.at[target],
            dst_ref=rbuf.at[me],
            send_sem=psend_sem.at[target],
            recv_sem=precv_sem.at[me],
            device_id=(target // 16, target % 16),
            device_id_type=MESH,
        )

    def piece_in(origin):
        return pltpu.make_async_remote_copy(
            src_ref=rbuf.at[origin],
            dst_ref=rbuf.at[origin],
            send_sem=psend_sem.at[origin],
            recv_sem=precv_sem.at[origin],
            device_id=(origin // 16, origin % 16),
            device_id_type=MESH,
        )

    def triple_of(part, number_):
        return 4 * part + (part + number_) % 4

    def finish(number_, _):
        modes_i = [3 * triple_of(part, number_) + e for part in range(4) for e in range(3)]
        for n in range(8):
            lines = lines_of(n % 4, 3 * (n // 4))
            sums = lax.dot_general(
                products(modes_i, lines, uv, last_g.at[n]),
                advected(1, lines, uc),
                NT,
                preferred_element_type=f32,
            )
            for part in range(4):
                first = pl.multiple_of(144 * triple_of(part, number_), 8)
                conv[pl.ds(first, 144), :] += sums[part * 144 : part * 144 + 144]
        for phase in range(4):

            @pl.when(number_ == phase)
            def _():
                total = viscous_end(phase)
                if phase < 3:
                    viscous_start(phase + 1, total)
                else:
                    diss_out[...] = total * scales[1]

        for part in range(4):
            for e in range(3):
                first = pl.multiple_of(144 * triple_of(part, number_) + 48 * e, 8)
                turned[part * 144 + e * 48 : part * 144 + e * 48 + 48, :] = jnp.transpose(
                    conv[pl.ds(first, 48), :]
                )
        for part in range(4):
            for r in range(8):
                pieces[8 * triple_of(part, number_) + r] = packed(part * 144 + 18 * r)

        def send(n, _):
            target = 8 * triple_of((z + n) % 4, number_) + (me + n // 4) % 8

            @pl.when(target != me)
            def _():
                piece_out(target).start()

            @pl.when(target == me)
            def _():
                rbuf[me] = pieces[me]

            return 0

        lax.fori_loop(0, 32, send, 0)
        return 0

    lax.fori_loop(0, 4, finish, 0)

    def wait_piece(origin, _):
        @pl.when(origin != me)
        def _():
            piece_in(origin).wait_recv()

        return 0

    lax.fori_loop(0, 128, wait_piece, 0)

    def gather(n, running):
        return running + rbuf[n]

    summed = lax.fori_loop(0, 128, gather, jnp.zeros((8, 128), f32)) * scales[0]
    conv_out[0:8, :] = summed[:, :48]
    conv_out[8:16, :] = pltpu.roll(summed, 80, 1)[:, :48]
    ends = jnp.zeros((8, 128), f32)
    for third in range(3):
        piece = pltpu.roll(summed, 32 + 16 * third, 1)
        piece = pltpu.roll(piece, 8 - 2 * third, 0) if third else piece
        ends = jnp.where((lane >= 16 * third) & (lane < 16 * third + 16), piece, ends)
    conv_out[16:18, :] = ends[:2, :48]

    def wait_out(n, _):
        copy_out(n // 31, n % 31 + 1).wait_send()
        return 0

    lax.fori_loop(0, 31 * CHUNKS, wait_out, 0)
    for index in range(4):
        other = number_of(home(index)) != number

        @pl.when(other)
        def _():
            volume_out(index).wait_send()

    for side in range(2):

        @pl.when(neighbours[side][0])
        def _():
            for chunk in range(CHUNKS):
                x_copy(side, chunk).wait_send()

        @pl.when(neighbours[2 + side][0])
        def _():
            y_copy(side).wait_send()

    for phase in range(4):
        for off in range(1, AXES[phase][1]):
            viscous_copy(phase, off, 1).wait_send()

    def wait_sent(target, _):
        @pl.when(target != me)
        def _():
            piece_out(target).wait_send()

        return 0

    lax.fori_loop(0, 128, wait_sent, 0)


def per_device(modes, volume):
    cell_total = 32 * 256 * 128
    scales = (1.0 / math.sqrt(cell_total), viscosity / cell_total)
    whole = pl.BlockSpec(memory_space=pltpu.VMEM)
    apart = pl.BlockSpec(memory_space=pl.ANY)
    dma = pltpu.SemaphoreType.DMA
    return pl.pallas_call(
        functools.partial(main_kernel, scales),
        out_shape=(
            jax.ShapeDtypeStruct((18, 48), f32),
            jax.ShapeDtypeStruct((48, 48), f32),
        ),
        in_specs=[apart, apart],
        out_specs=(whole, whole),
        scratch_shapes=[
            pltpu.VMEM((CHUNKS, 8, 4, 6, 3, 2, ROWS, 128), bf16),
            pltpu.VMEM((4, 8, 2, 128), f32),
            pltpu.VMEM((3, 12, 12, 48, 128), bf16),
            pltpu.VMEM((3, 8, 8, 48, 128), f32),
            pltpu.VMEM((48, 8, 128), f32),
            pltpu.VMEM((4, 3, 48, 512), bf16),
            pltpu.VMEM((4, 144, 512), bf16),
            pltpu.VMEM((8, 3, 48, 512), bf16),
            pltpu.VMEM((2304, 48), f32),
            pltpu.VMEM((144, 144), f32),
            pltpu.VMEM((584, 48), f32),
            pltpu.VMEM((128, 8, 128), f32),
            pltpu.VMEM((128, 8, 128), f32),
            pltpu.VMEM((4, 48, 48), f32),
            pltpu.VMEM((4, 4, 48, 48), f32),
            dma((CHUNKS, 32)),
            dma((CHUNKS, 32)),
            dma((4,)),
            dma((4,)),
            dma((2, CHUNKS)),
            dma((2, CHUNKS)),
            dma((2,)),
            dma((2,)),
            dma((CHUNKS + 1,)),
            dma((128,)),
            dma((128,)),
            dma((4, 4)),
            dma((4, 4)),
            pltpu.SemaphoreType.REGULAR,
        ],
        compiler_params=pltpu.CompilerParams(
            collective_id=0, has_side_effects=True, vmem_limit_bytes=56 << 20
        ),
    )(modes, volume)


def solution(mesh):
    placed = (P("mode", None, "slab", None, None), P(None, ("mode", "slab"), None))
    return jax.shard_map(
        per_device,
        mesh=mesh,
        in_specs=placed,
        out_specs=(P(("mode", "slab"), None), P()),
        check_vma=False,
    )
```

time: 112 us -> 101 us (0.902)
  the two profiles are of different devices: /device:TPU:0 before, /device:TPU:33 now
where the time goes in v3:
time: 101 us
  Pallas kernels  97.9 us (97%)
  local copies, waits for them, and re-layouts  2.65 us (3%)
    pallas_call x1, Pallas kernels, per_device(): pl.pallas_call(functools.partial(main_kernel, scales), out_shape=(jax.Sha...  97.9 us
    unnamed x2, local copies, waits for them, and re-layouts  2.65 us

profile of v3, /device:TPU:33, one launch (start us, length us, event | category | flops | bytes accessed | tf_op | source)
XLA Modules:
  0.0 101.2 jit_solution(7207635378451268524)
XLA Ops:
  0.6 97.9 %shard_map.41 = (f32[18,48]{1,0:T(8,128)}, f32[48,48]{1,0:T(8,128)}) custom-call(bf16[6,3,2,256,128]{4,3,2,1,0:T(8,128)(2,1)} %modes.1, f32[32,2,128]{2,1,0:T(2,128)} %volume.1), custom_call_target="tpu_custom_call" | custom-call | tf_op jit(solution)/shard_map/pallas_call | solution.py:598
  98.5 1.3 %copy.6 = f32[18,48]{1,0:T(8,128)} copy(f32[18,48]{1,0:T(8,128)} %get-tuple-element.4) | data formatting | bytes 6912
  99.8 1.3 %copy.7 = f32[48,48]{1,0:T(8,128)} copy(f32[48,48]{1,0:T(8,128)} %get-tuple-element.5) | data formatting | bytes 18432

commit v4 on v3

--- a/solution.py
+++ b/solution.py
@@ -128,9 +128,14 @@
     q = block_of(y, z, core)
     number = m * 16 + s
 
-    def peer(off, sign):
-        dz, dy, dc = off % 4, (off // 4) % 4, off // 16
-        return (y + sign * dy + 4) % 4, (z + sign * dz + 4) % 4, (core + dc) % 2
+    ys = [(y + dy) % 4 for dy in range(4)]
+    zs = [(z + dz) % 4 for dz in range(4)]
+    cores = [core, 1 - core]
+    offsets = [(n * 11) % 32 for n in range(1, 32)]
+    peers = []
+    for off in offsets:
+        py, pz, pc = ys[(off // 4) % 4], zs[off % 4], cores[off // 16]
+        peers.append((8 * block_of(py, pz, pc), device(x, py, pz, pc)))
 
     def home(index):
         return (index,) + owner_of(4 * m + s // 4)
@@ -151,13 +156,8 @@
 
     barrier = pltpu.get_barrier_semaphore()
 
-    def greet(off, _):
-        pl.semaphore_signal(
-            barrier, inc=1, device_id=device(x, *peer(off, 1)), device_id_type=MESH
-        )
-        return 0
-
-    lax.fori_loop(1, 32, greet, 0)
+    for _, other in peers:
+        pl.semaphore_signal(barrier, inc=1, device_id=other, device_id_type=MESH)
     for step in range(1, 4):
         pl.semaphore_signal(
             barrier, inc=1, device_id=device((x + step) % 4, y, z, core), device_id_type=MESH
@@ -204,34 +204,32 @@
             device_id_type=MESH,
         )
 
-    def copy_out(chunk, off):
-        py, pz, pc = peer(off, 1)
-        first = pl.multiple_of(8 * block_of(py, pz, pc) + ROWS * chunk, ROWS)
-        return pltpu.make_async_remote_copy(
-            src_ref=modes.at[:, :, :, pl.ds(first, ROWS), :],
-            dst_ref=recv.at[chunk, m, t],
-            send_sem=send_sem.at[chunk, off],
-            recv_sem=recv_sem.at[chunk, off],
-            device_id=device(x, py, pz, pc),
-            device_id_type=MESH,
-        )
-
-    def copy_in(chunk, off):
-        py, pz, pc = peer(off, -1)
-        slot = recv.at[chunk, pz * 2 + py // 2, (py % 2) * 2 + pc]
-        return pltpu.make_async_remote_copy(
-            src_ref=slot,
-            dst_ref=slot,
-            send_sem=send_sem.at[chunk, off],
-            recv_sem=recv_sem.at[chunk, off],
-            device_id=device(x, py, pz, pc),
+    def copy_out(chunk, first, other):
+        rows = pl.multiple_of(first + ROWS * chunk, ROWS)
+        return pltpu.make_async_remote_copy(
+            src_ref=modes.at[:, :, :, pl.ds(rows, ROWS), :],
+            dst_ref=recv.at[chunk, 4 * m + t],
+            send_sem=send_sem.at[chunk],
+            recv_sem=recv_sem.at[chunk],
+            device_id=other,
+            device_id_type=MESH,
+        )
+
+    def part_of(chunk):
+        slots = recv.at[chunk, pl.ds(0, 31)]
+        return pltpu.make_async_remote_copy(
+            src_ref=slots,
+            dst_ref=slots,
+            send_sem=send_sem.at[chunk],
+            recv_sem=recv_sem.at[chunk],
+            device_id=peers[0][1],
             device_id_type=MESH,
         )
 
     def copy_own(chunk):
         first = pl.multiple_of(8 * q + ROWS * chunk, ROWS)
         return pltpu.make_async_copy(
-            modes.at[:, :, :, pl.ds(first, ROWS), :], recv.at[chunk, m, t], own_sem.at[chunk]
+            modes.at[:, :, :, pl.ds(first, ROWS), :], recv.at[chunk, 4 * m + t], own_sem.at[chunk]
         )
 
     @pl.when(own_volume)
@@ -264,11 +262,9 @@
         def _():
             volume_out(index).start()
 
-    def start_out(n, _):
-        copy_out(n // 31, n % 31 + 1).start()
-        return 0
-
-    lax.fori_loop(0, 31 * CHUNKS, start_out, 0)
+    for chunk in range(CHUNKS):
+        for first, other in peers:
+            copy_out(chunk, first, other).start()
 
     for index in range(4):
         origin = source(index)
@@ -329,19 +325,16 @@
         )
 
     def arrive(chunk):
-        def wait_in(off, _):
-            copy_in(chunk, off).wait_recv()
-            return 0
-
-        lax.fori_loop(1, 32, wait_in, 0)
+        part_of(chunk).wait_recv()
         copy_own(chunk).wait()
 
         def turn(n, _):
             a = n // 8
             plane = n % 8
-            wide[:, 0:ROWS, :] = (
-                recv[chunk, :, plane // 2, :, a, plane % 2].astype(f32).reshape(48, ROWS, 128)
-            )
+            for six in range(8):
+                wide[6 * six : 6 * six + 6, 0:ROWS, :] = recv[
+                    chunk, 4 * six + plane // 2, :, a, plane % 2
+                ].astype(f32)
             for row in range(ROWS):
                 here = ROWS * chunk + row
                 field = wide.reshape(384, 128)[pl.ds(row, 48, stride=8), :]
@@ -385,9 +378,9 @@
 
             work(0, chunk - 1)
 
-        @pl.when(jnp.logical_or(chunk == 2, chunk == 4))
-        def _():
-            work(1, chunk // 2)
+        @pl.when(chunk == 2)
+        def _():
+            work(1, 1)
 
         return 0
 
@@ -399,14 +392,15 @@
         def _():
             y_arrival(side).wait_recv()
 
-    def last_slopes(half, _):
+    def last_slopes(part, _):
+        pair = part + (part + 1) // 2
         for n in range(4):
-            slot = last_g.at[4 * half + n]
-            slopes(1, n, 3 * half, uc, vrecv, slot, gw.at[n])
+            slot = last_g.at[4 * part + n]
+            slopes(1, n, pair, uc, vrecv, slot, gw.at[n])
             viscous(slot, gw.at[n], diss)
         return 0
 
-    lax.fori_loop(0, 2, last_slopes, 0)
+    lax.fori_loop(0, 3, last_slopes, 0)
 
     here = (x, y, z, core)
 
@@ -456,23 +450,23 @@
             tile = jnp.where((lane >= 96) & (lane < 112) & (line // 2 == third), ends, tile)
         return tile
 
-    def piece_out(target):
+    def piece_out(target, other):
         return pltpu.make_async_remote_copy(
             src_ref=pieces.at[target],
             dst_ref=rbuf.at[me],
-            send_sem=psend_sem.at[target],
-            recv_sem=precv_sem.at[me],
-            device_id=(target // 16, target % 16),
-            device_id_type=MESH,
-        )
-
-    def piece_in(origin):
-        return pltpu.make_async_remote_copy(
-            src_ref=rbuf.at[origin],
-            dst_ref=rbuf.at[origin],
-            send_sem=psend_sem.at[origin],
-            recv_sem=precv_sem.at[origin],
-            device_id=(origin // 16, origin % 16),
+            send_sem=psend_sem,
+            recv_sem=precv_sem,
+            device_id=other,
+            device_id_type=MESH,
+        )
+
+    def all_pieces():
+        return pltpu.make_async_remote_copy(
+            src_ref=pieces.at[pl.ds(0, 127)],
+            dst_ref=rbuf.at[pl.ds(0, 127)],
+            send_sem=psend_sem,
+            recv_sem=precv_sem,
+            device_id=peers[0][1],
             device_id_type=MESH,
         )
 
@@ -481,8 +475,8 @@
 
     def finish(number_, _):
         modes_i = [3 * triple_of(part, number_) + e for part in range(4) for e in range(3)]
-        for n in range(8):
-            lines = lines_of(n % 4, 3 * (n // 4))
+        for n in range(12):
+            lines = lines_of(n % 4, (0, 2, 3)[n // 4])
             sums = lax.dot_general(
                 products(modes_i, lines, uv, last_g.at[n]),
                 advected(1, lines, uc),
@@ -512,37 +506,31 @@
             for r in range(8):
                 pieces[8 * triple_of(part, number_) + r] = packed(part * 144 + 18 * r)
 
-        def send(n, _):
-            target = 8 * triple_of((z + n) % 4, number_) + (me + n // 4) % 8
-
-            @pl.when(target != me)
-            def _():
-                piece_out(target).start()
-
-            @pl.when(target == me)
-            def _():
-                rbuf[me] = pieces[me]
-
-            return 0
-
-        lax.fori_loop(0, 32, send, 0)
+        for step in range(8):
+            r = (s + step) % 8
+            for part in range(4):
+                triple = triple_of(zs[part], number_)
+                target = 8 * triple + r
+
+                @pl.when(target != me)
+                def _():
+                    piece_out(target, (triple // 2, 8 * (triple % 2) + r)).start()
+
+                @pl.when(target == me)
+                def _():
+                    rbuf[me] = pieces[me]
+
         return 0
 
     lax.fori_loop(0, 4, finish, 0)
 
-    def wait_piece(origin, _):
-        @pl.when(origin != me)
-        def _():
-            piece_in(origin).wait_recv()
-
-        return 0
-
-    lax.fori_loop(0, 128, wait_piece, 0)
+    all_pieces().wait_recv()
 
     def gather(n, running):
-        return running + rbuf[n]
-
-    summed = lax.fori_loop(0, 128, gather, jnp.zeros((8, 128), f32)) * scales[0]
+        return tuple(running[k] + rbuf[8 * n + k] for k in range(8))
+
+    sums = lax.fori_loop(0, 16, gather, (jnp.zeros((8, 128), f32),) * 8)
+    summed = sum(sums[1:], sums[0]) * scales[0]
     conv_out[0:8, :] = summed[:, :48]
     conv_out[8:16, :] = pltpu.roll(summed, 80, 1)[:, :48]
     ends = jnp.zeros((8, 128), f32)
@@ -552,11 +540,8 @@
         ends = jnp.where((lane >= 16 * third) & (lane < 16 * third + 16), piece, ends)
     conv_out[16:18, :] = ends[:2, :48]
 
-    def wait_out(n, _):
-        copy_out(n // 31, n % 31 + 1).wait_send()
-        return 0
-
-    lax.fori_loop(0, 31 * CHUNKS, wait_out, 0)
+    for chunk in range(CHUNKS):
+        part_of(chunk).wait_send()
     for index in range(4):
         other = number_of(home(index)) != number
 
@@ -579,14 +564,7 @@
         for off in range(1, AXES[phase][1]):
             viscous_copy(phase, off, 1).wait_send()
 
-    def wait_sent(target, _):
-        @pl.when(target != me)
-        def _():
-            piece_out(target).wait_send()
-
-        return 0
-
-    lax.fori_loop(0, 128, wait_sent, 0)
+    all_pieces().wait_send()
 
 
 def per_device(modes, volume):
@@ -604,14 +582,14 @@
         in_specs=[apart, apart],
         out_specs=(whole, whole),
         scratch_shapes=[
-            pltpu.VMEM((CHUNKS, 8, 4, 6, 3, 2, ROWS, 128), bf16),
+            pltpu.VMEM((CHUNKS, 32, 6, 3, 2, ROWS, 128), bf16),
             pltpu.VMEM((4, 8, 2, 128), f32),
             pltpu.VMEM((3, 12, 12, 48, 128), bf16),
             pltpu.VMEM((3, 8, 8, 48, 128), f32),
             pltpu.VMEM((48, 8, 128), f32),
             pltpu.VMEM((4, 3, 48, 512), bf16),
             pltpu.VMEM((4, 144, 512), bf16),
-            pltpu.VMEM((8, 3, 48, 512), bf16),
+            pltpu.VMEM((12, 3, 48, 512), bf16),
             pltpu.VMEM((2304, 48), f32),
             pltpu.VMEM((144, 144), f32),
             pltpu.VMEM((584, 48), f32),
@@ -619,8 +597,8 @@
             pltpu.VMEM((128, 8, 128), f32),
             pltpu.VMEM((4, 48, 48), f32),
             pltpu.VMEM((4, 4, 48, 48), f32),
-            dma((CHUNKS, 32)),
-            dma((CHUNKS, 32)),
+            dma((CHUNKS,)),
+            dma((CHUNKS,)),
             dma((4,)),
             dma((4,)),
             dma((2, CHUNKS)),
@@ -628,14 +606,14 @@
             dma((2,)),
             dma((2,)),
             dma((CHUNKS + 1,)),
-            dma((128,)),
-            dma((128,)),
+            dma,
+            dma,
             dma((4, 4)),
             dma((4, 4)),
             pltpu.SemaphoreType.REGULAR,
         ],
         compiler_params=pltpu.CompilerParams(
-            collective_id=0, has_side_effects=True, vmem_limit_bytes=56 << 20
+            collective_id=0, has_side_effects=True, vmem_limit_bytes=36 << 20
         ),
     )(modes, volume)
 

time: 101 us -> 87.4 us (0.87)
  Pallas kernels: 97.9 us -> 82.9 us
    pallas_call x1, Pallas kernels: 97.9 us -> 82.9 us  [per_device(): pl.pallas_call(functools.partial(main_kernel, scales), out_shape=(jax.Sha...]
    unnamed x2 -> x6, local copies, waits for them, and re-layouts: 2.65 us -> 3.63 us
where the time goes in v4:
time: 87.4 us; the launch traced here: 87.2 us
  Pallas kernels  82.9 us (95%)
  local copies, waits for them, and re-layouts  3.63 us (4%)
    pallas_call x1, Pallas kernels, per_device(): pl.pallas_call(functools.partial(main_kernel, scales), out_shape=(jax.Sha...  82.9 us
    unnamed x6, local copies, waits for them, and re-layouts  3.63 us

profile of v4, /device:TPU:33, one launch (start us, length us, event | category | flops | bytes accessed | tf_op | source)
XLA Modules:
  0.0 87.2 jit_solution(17235974460439363396)
XLA Ops:
  0.6 0.0 copy-start
  0.6 1.7 %copy-done = bf16[6,3,2,256,128]{4,3,2,1,0:T(8,128)(2,1)S(1)} copy-done((bf16[6,3,2,256,128]{4,3,2,1,0:T(8,128)(2,1)S(1)}, bf16[6,3,2,256,128]{4,3,2,1,0:T(8,128)(2,1)}, u32[]{:S(2)}) %copy-start) | copy-done | bytes 2359320
  2.3 0.0 copy-start.1
  2.3 0.8 copy-done.1
  3.1 82.9 %shard_map.41 = (f32[18,48]{1,0:T(8,128)S(1)}, f32[48,48]{1,0:T(8,128)S(1)}) custom-call(bf16[6,3,2,256,128]{4,3,2,1,0:T(8,128)(2,1)S(1)} %copy-done, f32[32,2,128]{2,1,0:T(2,128)S(1)} %copy-done.1), custom_call_target="tpu_custom_call" | custom-call | tf_op jit(solution)/shard_map/pallas_call | solution.py:576
  86.0 0.6 copy.6
  86.6 0.6 copy.7
Async XLA Ops:
  0.6 1.7 %copy-start = (bf16[6,3,2,256,128]{4,3,2,1,0:T(8,128)(2,1)S(1)}, bf16[6,3,2,256,128]{4,3,2,1,0:T(8,128)(2,1)}, u32[]{:S(2)}) copy-start(bf16[6,3,2,256,128]{4,3,2,1,0:T(8,128)(2,1)} %modes.1) | copy-start | bytes 7077892
  2.3 0.8 copy-start.1

commit v5 on v4

--- a/solution.py
+++ b/solution.py
@@ -107,12 +107,12 @@
     viscous(g, gw, diss)
 
 
-def four_units(b, pair, uc, uv, vrecv, g, gw, conv, diss):
-    slopes(b, 0, pair, uc, vrecv, g.at[0], gw.at[0])
-    for n in range(4):
-        if n < 3:
-            slopes(b, n + 1, pair, uc, vrecv, g.at[n + 1], gw.at[n + 1])
-        contract(b, n, pair, uc, uv, g.at[n], gw.at[n], conv, diss)
+def units(spots, uc, uv, vrecv, g, gw, conv, diss):
+    slopes(*spots[0], uc, vrecv, g.at[0], gw.at[0])
+    for n, spot in enumerate(spots):
+        if n + 1 < len(spots):
+            slopes(*spots[n + 1], uc, vrecv, g.at[n + 1], gw.at[n + 1])
+        contract(*spot, uc, uv, g.at[n], gw.at[n], conv, diss)
 
 
 def main_kernel(
@@ -328,22 +328,22 @@
         part_of(chunk).wait_recv()
         copy_own(chunk).wait()
 
-        def turn(n, _):
-            a = n // 8
-            plane = n % 8
-            for six in range(8):
-                wide[6 * six : 6 * six + 6, 0:ROWS, :] = recv[
-                    chunk, 4 * six + plane // 2, :, a, plane % 2
-                ].astype(f32)
-            for row in range(ROWS):
-                here = ROWS * chunk + row
-                field = wide.reshape(384, 128)[pl.ds(row, 48, stride=8), :]
-                uc[a, plane + 2, here + 2] = field.astype(bf16)
-                weight = vrecv[here // 2, plane, pl.ds(here % 2, 1), :].reshape(1, 128)
-                uv[a, plane, here] = field * weight
+        def turn(plane, _):
+            for a in range(3):
+                for six in range(8):
+                    wide[a, 6 * six : 6 * six + 6, 0:ROWS, :] = recv[
+                        chunk, 4 * six + plane // 2, :, a, plane % 2
+                    ].astype(f32)
+            for a in range(3):
+                for row in range(ROWS):
+                    here = ROWS * chunk + row
+                    field = wide.at[a].reshape(384, 128)[pl.ds(row, 48, stride=8), :]
+                    uc[a, plane + 2, here + 2] = field.astype(bf16)
+                    weight = vrecv[here // 2, plane, pl.ds(here % 2, 1), :].reshape(1, 128)
+                    uv[a, plane, here] = field * weight
             return 0
 
-        lax.fori_loop(0, 24, turn, 0)
+        lax.fori_loop(0, 8, turn, 0)
 
         for side in range(2):
 
@@ -359,14 +359,14 @@
         def _():
             y_copy(1).start()
 
-    def work(b, pair):
-        four_units(b, pair, uc, uv, vrecv, g, gw, conv, diss)
+    def work(*spots):
+        units(spots, uc, uv, vrecv, g, gw, conv, diss)
 
     def advance(chunk, _):
         @pl.when(chunk < CHUNKS)
         def _():
             arrive(chunk)
-            work(2, chunk)
+            work(*[(2, column, chunk) for column in range(4)], (0, 1, chunk), (0, 2, chunk))
 
         @pl.when(chunk >= 1)
         def _():
@@ -376,11 +376,11 @@
                 def _():
                     x_arrival(side, chunk - 1).wait_recv()
 
-            work(0, chunk - 1)
+            work((0, 0, chunk - 1), (0, 3, chunk - 1))
 
         @pl.when(chunk == 2)
         def _():
-            work(1, 1)
+            work(*[(1, column, 1) for column in range(4)])
 
         return 0
 
@@ -586,9 +586,9 @@
             pltpu.VMEM((4, 8, 2, 128), f32),
             pltpu.VMEM((3, 12, 12, 48, 128), bf16),
             pltpu.VMEM((3, 8, 8, 48, 128), f32),
-            pltpu.VMEM((48, 8, 128), f32),
-            pltpu.VMEM((4, 3, 48, 512), bf16),
-            pltpu.VMEM((4, 144, 512), bf16),
+            pltpu.VMEM((3, 48, 8, 128), f32),
+            pltpu.VMEM((6, 3, 48, 512), bf16),
+            pltpu.VMEM((6, 144, 512), bf16),
             pltpu.VMEM((12, 3, 48, 512), bf16),
             pltpu.VMEM((2304, 48), f32),
             pltpu.VMEM((144, 144), f32),
@@ -613,7 +613,7 @@
             pltpu.SemaphoreType.REGULAR,
         ],
         compiler_params=pltpu.CompilerParams(
-            collective_id=0, has_side_effects=True, vmem_limit_bytes=36 << 20
+            collective_id=0, has_side_effects=True, vmem_limit_bytes=53 << 20
         ),
     )(modes, volume)
 

time: 87.4 us -> 83 us (0.950)
  Pallas kernels: 82.9 us -> 80.2 us
  local copies, waits for them, and re-layouts: 3.63 us -> 1.96 us
    pallas_call x1, Pallas kernels: 82.9 us -> 80.2 us  [per_device(): pl.pallas_call(functools.partial(main_kernel, scales), out_shape=(jax.Sha...]
    unnamed x6 -> x4, local copies, waits for them, and re-layouts: 3.63 us -> 1.96 us
where the time goes in v5:
time: 83 us; the launch traced here: 82.8 us
  Pallas kernels  80.2 us (97%)
  local copies, waits for them, and re-layouts  1.96 us (2%)
    pallas_call x1, Pallas kernels, per_device(): pl.pallas_call(functools.partial(main_kernel, scales), out_shape=(jax.Sha...  80.2 us
    unnamed x4, local copies, waits for them, and re-layouts  1.96 us

profile of v5, /device:TPU:33, one launch (start us, length us, event | category | flops | bytes accessed | tf_op | source)
XLA Modules:
  0.0 82.8 jit_solution(6798873382787666461)
XLA Ops:
  0.6 0.0 copy-start
  0.6 0.7 copy-done
  1.4 80.2 %shard_map.41 = (f32[18,48]{1,0:T(8,128)S(1)}, f32[48,48]{1,0:T(8,128)S(1)}) custom-call(bf16[6,3,2,256,128]{4,3,2,1,0:T(8,128)(2,1)} %modes.1, f32[32,2,128]{2,1,0:T(2,128)S(1)} %copy-done), custom_call_target="tpu_custom_call" | custom-call | tf_op jit(solution)/shard_map/pallas_call | solution.py:576
  81.6 0.6 copy.6
  82.2 0.6 copy.7
Async XLA Ops:
  0.6 0.8 copy-start

commit v6 on v5

--- a/solution.py
+++ b/solution.py
@@ -255,6 +255,9 @@
             ready_sem, inc=1, device_id=device((x + step) % 4, y, z, core), device_id_type=MESH
         )
 
+    for first, other in peers:
+        copy_out(0, first, other).start()
+
     for index in range(4):
         other = number_of(home(index)) != number
 
@@ -262,7 +265,7 @@
         def _():
             volume_out(index).start()
 
-    for chunk in range(CHUNKS):
+    for chunk in range(1, CHUNKS):
         for first, other in peers:
             copy_out(chunk, first, other).start()
 
@@ -386,21 +389,21 @@
 
     lax.fori_loop(0, CHUNKS + 1, advance, 0)
 
+    def last_slopes(*parts):
+        for n in range(4 * len(parts)):
+            part = parts[n // 4]
+            slot = last_g.at[4 * part + n % 4]
+            slopes(1, n % 4, (0, 2, 3)[part], uc, vrecv, slot, gw.at[n % 6])
+            viscous(slot, gw.at[n % 6], diss)
+
+    last_slopes(1)
     for side in range(2):
 
         @pl.when(neighbours[2 + side][0])
         def _():
             y_arrival(side).wait_recv()
 
-    def last_slopes(part, _):
-        pair = part + (part + 1) // 2
-        for n in range(4):
-            slot = last_g.at[4 * part + n]
-            slopes(1, n, pair, uc, vrecv, slot, gw.at[n])
-            viscous(slot, gw.at[n], diss)
-        return 0
-
-    lax.fori_loop(0, 3, last_slopes, 0)
+    last_slopes(0, 2)
 
     here = (x, y, z, core)
 

time: 83 us -> 82.9 us (level)
  no operation moved by 1% of the time
where the time goes in v6:
time: 82.9 us; the launch traced here: 82.7 us
  Pallas kernels  80.1 us (97%)
  local copies, waits for them, and re-layouts  1.96 us (2%)
    pallas_call x1, Pallas kernels, per_device(): pl.pallas_call(functools.partial(main_kernel, scales), out_shape=(jax.Sha...  80.1 us
    unnamed x4, local copies, waits for them, and re-layouts  1.96 us

profile of v6, /device:TPU:33, one launch (start us, length us, event | category | flops | bytes accessed | tf_op | source)
XLA Modules:
  0.0 82.7 jit_solution(1666533738807332933)
XLA Ops:
  0.6 0.0 copy-start
  0.6 0.7 copy-done
  1.4 80.1 %shard_map.41 = (f32[18,48]{1,0:T(8,128)S(1)}, f32[48,48]{1,0:T(8,128)S(1)}) custom-call(bf16[6,3,2,256,128]{4,3,2,1,0:T(8,128)(2,1)} %modes.1, f32[32,2,128]{2,1,0:T(2,128)S(1)} %copy-done), custom_call_target="tpu_custom_call" | custom-call | tf_op jit(solution)/shard_map/pallas_call | solution.py:579
  81.5 0.6 copy.6
  82.1 0.6 copy.7
Async XLA Ops:
  0.6 0.8 copy-start
